TPU v7x, 32 devices: a whole 2x2x4 slice. The times are simulated.
32 devices in a mesh: blk: 4 (over y, x), row: 8 (over z, core).
Axes of the slice: x: 2, y: 2, z: 4, core: 2. Of those that a mesh axis runs over, the one named last changes fastest.
Arguments:
- inputs: float32 [16384, 512], P('row', 'blk'), may hold values from -30 to 30
- seq_lengths: int32 [8, 3], P('row'), may hold values from 1 to 1024, 2048 in all within a row
- poles: float32 [2, 2, 384], P(None, None, 'blk'), may hold values from -4 to 4, as said below
- log_step: float32 [2, 384], P(None, 'blk'), may hold values from -6.9 to -2.3
- in_matrix: float32 [2, 2, 384, 512], P(None, None, 'blk'), may hold values from -0.25 to 0.25
- out_matrix: float32 [2, 2, 384, 512], P(None, None, 'blk'), may hold values from -0.21875 to 0.21875
- feedthrough: float32 [2, 512], P(None, 'blk'), may hold values from -4 to 4
- norm_gain: float32 [2, 512], P(None, 'blk'), may hold values from 0.5 to 1.5
- norm_bias: float32 [2, 512], P(None, 'blk'), may hold values from -3 to 3
- cotangent: float32 [16384, 512], P('row', 'blk'), may hold values from -6 to 6
Outputs:
- outputs: float32 [16384, 512], P('row', 'blk')
- grad_inputs: float32 [16384, 512], P('row', 'blk')
- grad_poles: float32 [2, 2, 384], P(None, None, 'blk')
- grad_log_step: float32 [2, 384], P(None, 'blk')
- grad_in_matrix: float32 [2, 2, 384, 512], P(None, None, 'blk')
- grad_out_matrix: float32 [2, 2, 384, 512], P(None, None, 'blk')
- grad_feedthrough: float32 [2, 512], P(None, 'blk')
- grad_norm_gain: float32 [2, 512], P(None, 'blk')
- grad_norm_bias: float32 [2, 512], P(None, 'blk')
Inputs may be any that keep to these rules, and one draw needn't show every extreme that they name: `seq_lengths`: each packed row holds 3 sequences whose lengths sum to 2048; the longest of each row has exactly 1024 tokens. `poles`: the real parts are negative.
All inputs are finite; a program needn't handle non-finite values.
Results may differ from a plain program's by a relative error of at most 0.0003.
Values sent between devices are 32-bit elements; how exact they have to be, the bound alone decides.
A program may use at most 128 MiB of HBM per device.

v0:
```python
import jax
import jax.numpy as jnp
from jax import lax
from jax.sharding import PartitionSpec as P

EPSILON = 1e-05
PRECISE = lax.Precision.HIGHEST


def product(matrix_left, matrix_right):
    return jnp.dot(matrix_left, matrix_right, precision=PRECISE, preferred_element_type=jnp.float32)


def contract_rows(matrix_left, matrix_right):
    return lax.dot_general(
        matrix_left,
        matrix_right,
        (((0,), (0,)), ((), ())),
        precision=PRECISE,
        preferred_element_type=jnp.float32,
    )


def contract_columns(matrix_left, matrix_right):
    return lax.dot_general(
        matrix_left,
        matrix_right,
        (((1,), (1,)), ((), ())),
        precision=PRECISE,
        preferred_element_type=jnp.float32,
    )


def discretize(pole_parts, log_steps, in_parts):
    step_sizes = jnp.exp(log_steps)
    decay_real = pole_parts[0] * step_sizes
    turn_imag = pole_parts[1] * step_sizes
    magnitude = jnp.exp(decay_real)
    lbar_real = magnitude * jnp.cos(turn_imag)
    lbar_imag = magnitude * jnp.sin(turn_imag)
    modulus = pole_parts[0] * pole_parts[0] + pole_parts[1] * pole_parts[1]
    factor_real = ((lbar_real - 1.0) * pole_parts[0] + lbar_imag * pole_parts[1]) / modulus
    factor_imag = (lbar_imag * pole_parts[0] - (lbar_real - 1.0) * pole_parts[1]) / modulus
    drive_real = factor_real[:, None] * in_parts[0] - factor_imag[:, None] * in_parts[1]
    drive_imag = factor_real[:, None] * in_parts[1] + factor_imag[:, None] * in_parts[0]
    return (lbar_real, lbar_imag, jnp.concatenate([drive_real, drive_imag], axis=0))


def compose(earlier, later):
    return (
        later[0] * earlier[0] - later[1] * earlier[1],
        later[0] * earlier[1] + later[1] * earlier[0],
        later[0] * earlier[2] - later[1] * earlier[3] + later[2],
        later[0] * earlier[3] + later[1] * earlier[2] + later[3],
    )


def block_scan(keep_flags, coef_real, coef_imag, drive_real, drive_imag, backward):
    token_total = keep_flags.shape[0]
    state_count = coef_real.shape[0]
    block_total = 128
    step_total = token_total // block_total
    flag_grid = keep_flags.reshape(block_total, step_total).T

    def arrange(values):
        return values.reshape(block_total, step_total, state_count).transpose(1, 2, 0)

    def advance(carry, item):
        acc_real, acc_imag, run_real, run_imag = carry
        flag_row, push_real, push_imag = item
        gate_real = coef_real[:, None] * flag_row[None, :]
        gate_imag = coef_imag[:, None] * flag_row[None, :]
        updated = (
            gate_real * acc_real - gate_imag * acc_imag,
            gate_real * acc_imag + gate_imag * acc_real,
            gate_real * run_real - gate_imag * run_imag + push_real,
            gate_real * run_imag + gate_imag * run_real + push_imag,
        )
        return (updated, updated)

    ones_grid = jnp.ones((state_count, block_total), jnp.float32)
    zero_grid = jnp.zeros((state_count, block_total), jnp.float32)
    totals, history = lax.scan(
        advance,
        (ones_grid, zero_grid, zero_grid, zero_grid),
        (flag_grid, arrange(drive_real), arrange(drive_imag)),
        reverse=backward,
    )
    summary = lax.associative_scan(compose, totals, reverse=backward, axis=1)
    ones_col = jnp.ones((state_count, 1), jnp.float32)
    zero_col = jnp.zeros((state_count, 1), jnp.float32)
    fills = (ones_col, zero_col, zero_col, zero_col)
    if backward:
        entering = [
            jnp.concatenate([member[:, 1:], fill], axis=1) for member, fill in zip(summary, fills)
        ]
    else:
        entering = [
            jnp.concatenate([fill, member[:, :-1]], axis=1) for member, fill in zip(summary, fills)
        ]
    enter_acc_real = entering[0][None]
    enter_acc_imag = entering[1][None]
    enter_real = entering[2][None]
    enter_imag = entering[3][None]
    hist_acc_real, hist_acc_imag, hist_real, hist_imag = history
    full_acc_real = hist_acc_real * enter_acc_real - hist_acc_imag * enter_acc_imag
    full_acc_imag = hist_acc_real * enter_acc_imag + hist_acc_imag * enter_acc_real
    full_real = hist_real + hist_acc_real * enter_real - hist_acc_imag * enter_imag
    full_imag = hist_imag + hist_acc_real * enter_imag + hist_acc_imag * enter_real

    def restore(values):
        return values.transpose(2, 0, 1).reshape(token_total, state_count)

    return (restore(full_acc_real), restore(full_acc_imag), restore(full_real), restore(full_imag))


def linear_scan(keep_flags, coef_real, coef_imag, drive_real, drive_imag, backward):
    result = block_scan(keep_flags, coef_real, coef_imag, drive_real, drive_imag, backward)
    return (result[2], result[3])


def boundary_flags(seq_lengths, row_tokens):
    seq_ends = jnp.cumsum(seq_lengths, axis=1)
    begins = seq_ends - seq_lengths
    positions = jnp.arange(row_tokens, dtype=jnp.int32)
    matches = positions[None, :, None] == begins[:, None, :]
    return jnp.any(matches, axis=2).astype(jnp.float32)


def activation(mixed_out):
    return jax.nn.gelu(mixed_out, approximate=False) * jax.nn.sigmoid(mixed_out)


def previous_states(states, backward):
    padding = jnp.zeros((1, states.shape[1]), jnp.float32)
    if backward:
        return jnp.concatenate([states[1:], padding], axis=0)
    return jnp.concatenate([padding, states[:-1]], axis=0)


def layer_forward(hidden, weights, keep_flags, backward, token_count):
    pole_parts, log_steps, in_parts, out_parts, feed_gain, norm_scale, norm_shift = weights
    totals = lax.psum((jnp.sum(hidden, axis=0), jnp.sum(hidden * hidden, axis=0)), "row")
    feature_mean = totals[0] / token_count
    feature_square = totals[1] / token_count
    inv_scale = lax.rsqrt(feature_square - feature_mean * feature_mean + EPSILON)
    centred = (hidden - feature_mean) * inv_scale
    normed = norm_scale * centred + norm_shift
    lbar_real, lbar_imag, drive_matrix = discretize(pole_parts, log_steps, in_parts)
    state_count = lbar_real.shape[0]
    mixing = jnp.concatenate([2.0 * out_parts[0], -2.0 * out_parts[1]], axis=0)
    edge_values = None
    normed_all = lax.all_gather(normed, "blk", axis=1, tiled=True)
    drive_terms = contract_columns(normed_all, drive_matrix)
    state_real, state_imag = linear_scan(
        keep_flags,
        lbar_real,
        lbar_imag,
        drive_terms[:, :state_count],
        drive_terms[:, state_count:],
        backward,
    )
    states = jnp.concatenate([state_real, state_imag], axis=1)
    partial_out = product(states, mixing)
    mixed_out = lax.psum_scatter(partial_out, "blk", scatter_dimension=1, tiled=True)
    mixed_out = mixed_out + feed_gain * normed
    saved_values = (normed, normed_all, centred, inv_scale, states, mixed_out, edge_values)
    return (hidden + activation(mixed_out), saved_values)


def layer_backward(grad_out, saved_values, weights, keep_flags, keep_other, backward, token_count):
    normed, normed_all, centred, inv_scale, states, mixed_out, edge_values = saved_values
    pole_parts, log_steps, in_parts, out_parts, feed_gain, norm_scale, norm_shift = weights
    activation_back = jax.vjp(activation, mixed_out)[1]
    grad_mixed = activation_back(grad_out)[0]
    grad_feed = jnp.sum(grad_mixed * normed, axis=0)
    grad_mixed_all = lax.all_gather(grad_mixed, "blk", axis=1, tiled=True)
    lbar_real, lbar_imag, drive_matrix = discretize(pole_parts, log_steps, in_parts)
    state_count = lbar_real.shape[0]
    mixing = jnp.concatenate([2.0 * out_parts[0], -2.0 * out_parts[1]], axis=0)
    grad_mixing = contract_rows(states, grad_mixed_all)
    grad_out_parts = jnp.stack([2.0 * grad_mixing[:state_count], -2.0 * grad_mixing[state_count:]])
    seeds = contract_columns(grad_mixed_all, mixing)
    adjoint_real, adjoint_imag = linear_scan(
        keep_other,
        lbar_real,
        -lbar_imag,
        seeds[:, :state_count],
        seeds[:, state_count:],
        not backward,
    )
    adjoint = jnp.concatenate([adjoint_real, adjoint_imag], axis=1)
    adjoint_real = adjoint[:, :state_count]
    adjoint_imag = adjoint[:, state_count:]
    before = previous_states(states, backward)
    before_real = before[:, :state_count]
    before_imag = before[:, state_count:]
    grad_lbar_real = jnp.sum(
        keep_flags[:, None] * (adjoint_real * before_real + adjoint_imag * before_imag), axis=0
    )
    grad_lbar_imag = jnp.sum(
        keep_flags[:, None] * (adjoint_imag * before_real - adjoint_real * before_imag), axis=0
    )
    grad_drive = contract_rows(adjoint, normed_all)
    partial_grad = product(adjoint, drive_matrix)
    grad_normed = lax.psum_scatter(partial_grad, "blk", scatter_dimension=1, tiled=True)
    grad_normed = grad_normed + feed_gain * grad_mixed
    discretize_back = jax.vjp(discretize, pole_parts, log_steps, in_parts)[1]
    grad_poles, grad_steps, grad_in_parts = discretize_back(
        (grad_lbar_real, grad_lbar_imag, grad_drive)
    )
    norm_totals = lax.psum(
        (jnp.sum(grad_normed, axis=0), jnp.sum(grad_normed * centred, axis=0)), "row"
    )
    grad_shift = norm_totals[0]
    grad_scale = norm_totals[1]
    grad_hidden = grad_out + norm_scale * inv_scale * (
        grad_normed - grad_shift / token_count - centred * grad_scale / token_count
    )
    return (
        grad_hidden,
        (grad_poles, grad_steps, grad_in_parts, grad_out_parts, grad_feed),
        grad_scale,
        grad_shift,
    )


def local(
    inputs,
    seq_lengths,
    poles,
    log_step,
    in_matrix,
    out_matrix,
    feedthrough,
    norm_gain,
    norm_bias,
    cotangent,
):
    row_tokens = inputs.shape[0] // seq_lengths.shape[0]
    token_count = inputs.shape[0] * lax.axis_size("row")
    start_flags = boundary_flags(seq_lengths, row_tokens).reshape(-1)
    keep_here = 1.0 - start_flags
    keep_next = jnp.concatenate([keep_here[1:], jnp.zeros((1,), jnp.float32)])
    pole_use, step_use, in_use, out_use = (poles, log_step, in_matrix, out_matrix)
    layer_weights = [
        (
            pole_use[layer_index],
            step_use[layer_index],
            in_use[layer_index],
            out_use[layer_index],
            feedthrough[layer_index],
            norm_gain[layer_index],
            norm_bias[layer_index],
        )
        for layer_index in range(2)
    ]
    keep_sets = [keep_here, keep_next]
    hidden = inputs
    saved_list = []
    for layer_index in range(2):
        hidden, saved_values = layer_forward(
            hidden,
            layer_weights[layer_index],
            keep_sets[layer_index],
            layer_index == 1,
            token_count,
        )
        saved_list.append(saved_values)
    grad_hidden = cotangent
    weight_grads = [None, None]
    scale_grads = [None, None]
    shift_grads = [None, None]
    for layer_index in (1, 0):
        grad_hidden, layer_grads, grad_scale, grad_shift = layer_backward(
            grad_hidden,
            saved_list[layer_index],
            layer_weights[layer_index],
            keep_sets[layer_index],
            keep_sets[1 - layer_index],
            layer_index == 1,
            token_count,
        )
        layer_grads = lax.psum(
            (layer_grads[0], layer_grads[1], layer_grads[2], layer_grads[3], layer_grads[4]), "row"
        )
        weight_grads[layer_index] = layer_grads
        scale_grads[layer_index] = grad_scale
        shift_grads[layer_index] = grad_shift
    stacked = [jnp.stack([weight_grads[0][member], weight_grads[1][member]]) for member in range(5)]
    return (
        hidden,
        grad_hidden,
        stacked[0],
        stacked[1],
        stacked[2],
        stacked[3],
        stacked[4],
        jnp.stack([scale_grads[0], scale_grads[1]]),
        jnp.stack([shift_grads[0], shift_grads[1]]),
    )


def solution(mesh):
    in_specs = (
        P("row", "blk"),
        P("row", None),
        P(None, None, "blk"),
        P(None, "blk"),
        P(None, None, "blk", None),
        P(None, None, "blk", None),
        P(None, "blk"),
        P(None, "blk"),
        P(None, "blk"),
        P("row", "blk"),
    )
    out_specs = (
        P("row", "blk"),
        P("row", "blk"),
        P(None, None, "blk"),
        P(None, "blk"),
        P(None, None, "blk", None),
        P(None, None, "blk", None),
        P(None, "blk"),
        P(None, "blk"),
        P(None, "blk"),
    )
    return jax.shard_map(local, mesh=mesh, in_specs=in_specs, out_specs=out_specs, check_vma=False)
```

profile of v0, /device:TPU:0, one launch (start us, length us, event | category | flops | bytes accessed | tf_op | source)
XLA Modules:
  0.0 1117.7 jit_solution(7443972019412569086)
XLA Ops:
  8.8 18.1 %all-reduce.149 = (f32[128]{0:T(128)S(1)}, f32[128]{0:T(128)S(1)}) all-reduce(f32[128]{0:T(128)S(1)} %get-tuple-element.1129, f32[128]{0:T(128)S(1)} %get-tuple-element.1128), channel_id=1, replica_groups=mesh['blk'=4,'row'=8] {'row'}, use_global_device_ids=true, to_apply=%region_5.6 | all-reduce | flops 256 | bytes 2048 | tf_op jit(solution)/shard_map/psum | solution.py:143
  29.5 2.4 multiply_add_fusion.9
  35.6 47.3 %all-gather.5.cloned.1.call-done = f32[2048,512]{1,0:T(8,128)} async-done(((f32[2048,128]{1,0:T(8,128)}), f32[2048,512]{1,0:T(8,128)}) %all-gather.5.cloned.1.call-update) | async-done | bytes 4194320 | tf_op jit(solution)/shard_map/all_gather | solution.py:153
  82.9 6.2 fusion.59
  95.9 24.9 %while.108 = (s32[]{:T(128)}, f32[96,128]{1,0:T(8,128)S(1)}, f32[96,128]{1,0:T(8,128)S(1)}, f32[96,128]{1,0:T(8,128)S(1)}, f32[96,128]{1,0:T(8,128)S(1)}, /*inde...) while((s32[]{:T(128)}, f32[96,128]{1,0:T(8,128)S(1)}, ...), condition=%wide.region_7.8_spmd.clone, body=%wide.region_6.7_spmd.clone.sunk | while | flops 245763 | bytes 690863 | solution.py:83
  126.9 6.3 fusion.37
  134.4 51.7 %reduce-scatter.5.cloned.1.call-done = f32[2048,128]{1,0:T(8,128)} async-done(((f32[2048,512]{1,0:T(8,128)}), f32[2048,128]{1,0:T(8,128)}) %reduce-scatter.5.cloned.1.call-update) | async-done | bytes 1048592 | tf_op jit(solution)/shard_map/reduce_scatter | solution.py:165
  186.1 3.8 fusion.160
  190.0 16.5 %all-reduce.148 = (f32[128]{0:T(128)S(1)}, f32[128]{0:T(128)S(1)}) all-reduce(f32[128]{0:T(128)S(1)} %get-tuple-element.1127, f32[128]{0:T(128)S(1)} %get-tuple-element.1126), channel_id=1, replica_groups=mesh['blk'=4,'row'=8] {'row'}, use_global_device_ids=true, to_apply=%region_12.13 | all-reduce | flops 256 | bytes 2048 | tf_op jit(solution)/shard_map/psum | solution.py:143
  209.5 48.7 %all-gather.7.cloned.1.call-done = f32[2048,512]{1,0:T(8,128)} async-done(((f32[2048,128]{1,0:T(8,128)}), f32[2048,512]{1,0:T(8,128)}) %all-gather.7.cloned.1.call-update) | async-done | bytes 4194320 | tf_op jit(solution)/shard_map/all_gather | solution.py:153
  258.2 6.2 fusion.57
  274.3 36.2 %while.109 = (s32[]{:T(128)}, f32[96,128]{1,0:T(8,128)S(1)}, f32[96,128]{1,0:T(8,128)S(1)}, f32[96,128]{1,0:T(8,128)S(1)}, f32[96,128]{1,0:T(8,128)S(1)}, /*inde...) while((s32[]{:T(128)}, f32[96,128]{1,0:T(8,128)S(1)}, ...), condition=%wide.region_14.15_spmd.clone, body=%wide.region_13.14_spmd.clone.sunk | while | flops 245764 | bytes 690883 | solution.py:83
  350.5 3.0 subtract_bitcast_fusion.2
  355.1 2.9 copy.192
  358.0 6.9 fusion.35
  364.9 10.1 all-gather.9.cloned.1.call-start
  375.1 42.7 %reduce-scatter.7.cloned.1.call-done = f32[2048,128]{1,0:T(8,128)} async-done(((f32[2048,512]{1,0:T(8,128)}), f32[2048,128]{1,0:T(8,128)}) %reduce-scatter.7.cloned.1.call-update) | async-done | bytes 1048592 | tf_op jit(solution)/shard_map/reduce_scatter | solution.py:165
  417.7 5.7 multiply_reduce_fusion
  423.5 52.6 %all-gather.9.cloned.1.call-done = f32[2048,512]{1,0:T(8,128)} async-done(((f32[2048,128]{1,0:T(8,128)}), f32[2048,512]{1,0:T(8,128)}) %all-gather.9.cloned.1.call-update) | async-done | bytes 4194320 | tf_op jit(solution)/shard_map/all_gather | solution.py:177
  476.2 6.3 fusion.56
  492.4 36.2 %while.110 = (s32[]{:T(128)}, f32[96,128]{1,0:T(8,128)S(1)}, f32[96,128]{1,0:T(8,128)S(1)}, f32[96,128]{1,0:T(8,128)S(1)}, f32[96,128]{1,0:T(8,128)S(1)}, /*inde...) while((s32[]{:T(128)}, f32[96,128]{1,0:T(8,128)S(1)}, ...), condition=%wide.region_17.18_spmd.clone, body=%wide.region_16.17_spmd.clone.sunk | while | flops 245763 | bytes 690863 | solution.py:83
  552.6 3.1 subtract_bitcast_fusion.1
  557.3 2.6 copy.215
  559.9 6.9 fusion.33
  566.9 52.7 %reduce-scatter.9.cloned.1.call-done = f32[2048,128]{1,0:T(8,128)} async-done(((f32[2048,512]{1,0:T(8,128)}), f32[2048,128]{1,0:T(8,128)}) %reduce-scatter.9.cloned.1.call-update) | async-done | bytes 1048592 | tf_op jit(solution)/shard_map/reduce_scatter | solution.py:206
  619.6 3.3 fusion.159
  622.9 17.1 %all-reduce.147 = (f32[128]{0:T(128)}, f32[128]{0:T(128)}) all-reduce(f32[128]{0:T(128)} %get-tuple-element.1125, f32[128]{0:T(128)} %get-tuple-element.1124), channel_id=1, replica_groups=mesh['blk'=4,'row'=8] {'row'}, use_global_device_ids=true, to_apply=%region_22.23 | all-reduce | flops 256 | bytes 2048 | tf_op jit(solution)/shard_map/psum | solution.py:212
  641.1 5.5 fusion.45
  646.8 11.2 %fusion.34 = f32[192,512]{1,0:T(8,128)S(1)} fusion(f32[2048,512]{1,0:T(8,128)} %all-gather.9.cloned.1.call-done, f32[2048,96]{1,0:T(8,128)} %bitcast.820, f32[2048,96]{1,0:T(8,128)} %bitcast.817), kind=kOutput, calls=%fused_computation.98 | convolution fusion | flops 2416312320 | bytes 6160384 | tf_op jit(solution)/shard_map/dot_general | solution.py:15
  659.4 5.9 fusion.32
  665.2 31.4 %all-gather.11.cloned.1.call-done = f32[2048,512]{1,0:T(8,128)} async-done(((f32[2048,128]{1,0:T(8,128)}), f32[2048,512]{1,0:T(8,128)}) %all-gather.11.cloned.1.call-update) | async-done | bytes 4194320 | tf_op jit(solution)/shard_map/all_gather | solution.py:177
  696.6 6.3 fusion.58
  704.1 2.4 copy.217
  706.6 2.5 copy.220
  709.1 2.4 copy.216
  711.5 2.5 copy.219
  718.0 39.1 %while.111 = (s32[]{:T(128)}, f32[96,128]{1,0:T(8,128)}, f32[96,128]{1,0:T(8,128)}, f32[96,128]{1,0:T(8,128)}, f32[96,128]{1,0:T(8,128)}, /*index=5*/f32[16,96,1...) while((s32[]{:T(128)}, f32[96,128]{1,0:T(8,128)}, ...), condition=%wide.region_24.25_spmd.clone, body=%wide.region_23.24_spmd.clone.sunk | while | flops 245764 | bytes 690627 | solution.py:83
  858.8 10.6 fusion.36
  944.1 3.3 subtract_bitcast_fusion
  947.4 2.6 copy.237
  950.0 2.5 copy.238
  952.5 10.7 fusion.30
  966.7 6.9 fusion.31
  980.1 49.0 %all-reduce.153.cloned.1.call-done = (f32[1,2,96,512]{3,2,1,0:T(8,128)}, f32[1,2,96,512]{3,2,1,0:T(8,128)}, f32[1,2,96,512]{3,2,1,0:T(8,128)}, f32[1,2,96,512]{3,2,1,0:T(8,128)}) async-done(((f32[1,2,96,512]{3,2,1,0:T(8,128)}, f32[1,2,96,512]{3,2,1,0:T(8,128)}, f32[1,2,96,512]{3,2,1,0:T(8,128)}, f32[1,2,96,512]{3,2,1,0:T(8,128)}), (f32[1,2,96,512]{3,2,1,0:T(8,128)}, f32[1,2,96,512]{3,2,1,0:T(8,128)}, ...) | async-done | bytes 1572880 | tf_op jit(solution)/shard_map/psum | solution.py:284
  1033.3 51.0 %reduce-scatter.11.cloned.1.call-done = f32[2048,128]{1,0:T(8,128)} async-done(((f32[2048,512]{1,0:T(8,128)}), f32[2048,128]{1,0:T(8,128)}) %reduce-scatter.11.cloned.1.call-update) | async-done | bytes 1048592 | tf_op jit(solution)/shard_map/reduce_scatter | solution.py:206
  1084.3 2.9 multiply_reduce_fusion.1
  1087.2 16.6 %all-reduce.146 = (f32[128]{0:T(128)S(1)}, f32[128]{0:T(128)S(1)}, f32[1,2,96]{2,1,0:T(2,128)S(1)}, f32[1,2,96]{2,1,0:T(2,128)S(1)}, f32[1,96]{1,0:T(1,128)S(1)}...) all-reduce(f32[128]{0:T(128)S(1)} %get-tuple-element.1122, ...), channel_id=1, replica_groups=mesh['blk'=4,'row'=8] {'row'}, use_global_device_ids=true, to_apply=%region_29.30 | all-reduce | flops 1088 | bytes 8704 | tf_op jit(solution)/shard_map/psum | solution.py:212
  1106.7 4.3 multiply_add_fusion
  (1069 shorter events, 447.3 us)
Async XLA Ops:
  7.2 75.7 %all-gather.5.cloned.1.call-start = ((), (), s32[]{:S(2)}) async-start(), calls=%async_computation.4 | async-start | bytes 5242880 | tf_op jit(solution)/shard_map/all_gather | solution.py:153
  32.0 154.1 %reduce-scatter.5.cloned.1.call-start = ((), (), s32[]{:S(2)}) async-start(), calls=%async_computation.5 | async-start | bytes 5242880 | tf_op jit(solution)/shard_map/reduce_scatter | solution.py:165
  32.4 176.2 %copy-start.32 = (f32[2048]{0:T(1024)}, f32[2048]{0:T(1024)S(1)}, u32[]{:S(2)}) copy-start(f32[2048]{0:T(1024)S(1)} %convert_subtract_fusion) | copy-start | bytes 24580
  33.2 56.0 %copy-start.43 = (f32[96]{0:T(128)}, f32[96]{0:T(128)S(1)}, u32[]{:S(2)}) copy-start(f32[96]{0:T(128)S(1)} %get-tuple-element.2127) | copy-start | bytes 1156
  33.7 55.4 %copy-start.83 = (f32[96]{0:T(128)}, f32[96]{0:T(128)S(1)}, u32[]{:S(2)}) copy-start(f32[96]{0:T(128)S(1)} %get-tuple-element.1326) | copy-start | bytes 1156
  33.8 55.4 %copy-start.77 = (f32[96]{0:T(128)}, f32[96]{0:T(128)S(1)}, u32[]{:S(2)}) copy-start(f32[96]{0:T(128)S(1)} %get-tuple-element.1329) | copy-start | bytes 1156
  33.8 55.4 %copy-start.79 = (f32[96]{0:T(128)}, f32[96]{0:T(128)S(1)}, u32[]{:S(2)}) copy-start(f32[96]{0:T(128)S(1)} %get-tuple-element.1637) | copy-start | bytes 1156
  33.8 55.4 %copy-start.81 = (f32[96]{0:T(128)}, f32[96]{0:T(128)S(1)}, u32[]{:S(2)}) copy-start(f32[96]{0:T(128)S(1)} %get-tuple-element.1638) | copy-start | bytes 1156
  34.7 92.2 %copy-start.17 = (f32[96,512]{1,0:T(8,128)}, f32[96,512]{1,0:T(8,128)S(1)}, u32[]{:S(2)}) copy-start(f32[96,512]{1,0:T(8,128)S(1)} %get-tuple-element.1386) | copy-start | bytes 589828
  133.2 52.9 %copy-start = (f32[2048,128]{1,0:T(8,128)S(1)}, f32[2048,128]{1,0:T(8,128)}, u32[]{:S(2)}) copy-start(f32[2048,128]{1,0:T(8,128)} %param.18) | copy-start | bytes 3145732
  133.2 52.9 %copy-start.56 = (f32[128]{0:T(128)S(1)}, f32[128]{0:T(128)}, u32[]{:S(2)}) copy-start(f32[128]{0:T(128)} %copy-done.55) | copy-start | bytes 1540
  133.2 52.9 %copy-start.60 = (f32[128]{0:T(128)S(1)}, f32[128]{0:T(128)}, u32[]{:S(2)}) copy-start(f32[128]{0:T(128)} %copy-done.59) | copy-start | bytes 1540
  133.3 52.9 %copy-start.63 = (f32[128]{0:T(128)S(1)}, f32[128]{0:T(128)}, u32[]{:S(2)}) copy-start(f32[128]{0:T(128)} %copy-done.62) | copy-start | bytes 1540
  133.3 52.9 %copy-start.66 = (f32[128]{0:T(128)S(1)}, f32[128]{0:T(128)}, u32[]{:S(2)}) copy-start(f32[128]{0:T(128)} %copy-done.65) | copy-start | bytes 1540
  133.3 73.2 %copy-start.89 = (f32[2,128]{1,0:T(2,128)S(1)}, f32[2,128]{1,0:T(2,128)}, u32[]{:S(2)}) copy-start(f32[2,128]{1,0:T(2,128)} %param.25) | copy-start | bytes 3076
  133.3 73.8 %copy-start.75 = (f32[128]{0:T(128)S(1)}, f32[128]{0:T(128)}, u32[]{:S(2)}) copy-start(f32[128]{0:T(128)} %get-tuple-element.1654) | copy-start | bytes 1540
  133.3 73.8 %copy-start.76 = (f32[128]{0:T(128)S(1)}, f32[128]{0:T(128)}, u32[]{:S(2)}) copy-start(f32[128]{0:T(128)} %get-tuple-element.1663) | copy-start | bytes 1540
  133.3 124.9 %all-gather.7.cloned.1.call-start = ((), (), s32[]{:S(2)}) async-start(), calls=%async_computation.6 | async-start | bytes 5242880 | tf_op jit(solution)/shard_map/all_gather | solution.py:153
  134.4 51.7 %copy-start.69 = (f32[128]{0:T(128)}, f32[128]{0:T(128)S(1)}, u32[]{:S(2)}) copy-start(f32[128]{0:T(128)S(1)} %get-tuple-element.1649) | copy-start | bytes 1540
  190.0 68.2 %copy-start.18 = (f32[96,512]{1,0:T(8,128)S(1)}, f32[96,512]{1,0:T(8,128)}, u32[]{:S(2)}) copy-start(f32[96,512]{1,0:T(8,128)} %get-tuple-element.1381) | copy-start | bytes 589828
  190.0 68.2 %copy-start.19 = (f32[96,512]{1,0:T(8,128)S(1)}, f32[96,512]{1,0:T(8,128)}, u32[]{:S(2)}) copy-start(f32[96,512]{1,0:T(8,128)} %get-tuple-element.1382) | copy-start | bytes 589828
  208.3 209.5 %reduce-scatter.7.cloned.1.call-start = ((), (), s32[]{:S(2)}) async-start(), calls=%async_computation.7 | async-start | bytes 5242880 | tf_op jit(solution)/shard_map/reduce_scatter | solution.py:165
  208.8 55.7 %copy-start.38 = (f32[2048]{0:T(1024)}, f32[2048]{0:T(1024)S(1)}, u32[]{:S(2)}) copy-start(f32[2048]{0:T(1024)S(1)} %pad_maximum_fusion.44) | copy-start | bytes 24580
  364.9 52.8 %copy-start.11 = (f32[2048,128]{1,0:T(8,128)S(1)}, f32[2048,128]{1,0:T(8,128)}, u32[]{:S(2)}) copy-start(f32[2048,128]{1,0:T(8,128)} %param.27) | copy-start | bytes 3145732
  364.9 52.8 %copy-start.47 = (f32[128]{0:T(128)S(1)}, f32[128]{0:T(128)}, u32[]{:S(2)}) copy-start(f32[128]{0:T(128)} %copy-done.46) | copy-start | bytes 1540
  364.9 52.8 %copy-start.51 = (f32[128]{0:T(128)S(1)}, f32[128]{0:T(128)}, u32[]{:S(2)}) copy-start(f32[128]{0:T(128)} %copy-done.50) | copy-start | bytes 1540
  364.9 111.2 %all-gather.9.cloned.1.call-start = ((), (), s32[]{:S(2)}) async-start(), calls=%async_computation.8 | async-start | bytes 5242880 | tf_op jit(solution)/shard_map/all_gather | solution.py:177
  423.4 196.2 %reduce-scatter.9.cloned.1.call-start = ((), (), s32[]{:S(2)}) async-start(), calls=%async_computation.9 | async-start | bytes 5242880 | tf_op jit(solution)/shard_map/reduce_scatter | solution.py:206
  566.8 52.8 %copy-start.48 = (f32[128]{0:T(128)S(1)}, f32[128]{0:T(128)}, u32[]{:S(2)}) copy-start(f32[128]{0:T(128)} %copy-done.46) | copy-start | bytes 1540
  566.8 52.8 %copy-start.52 = (f32[128]{0:T(128)S(1)}, f32[128]{0:T(128)}, u32[]{:S(2)}) copy-start(f32[128]{0:T(128)} %copy-done.50) | copy-start | bytes 1540
  566.8 74.3 %copy-start.57 = (f32[128]{0:T(128)S(1)}, f32[128]{0:T(128)}, u32[]{:S(2)}) copy-start(f32[128]{0:T(128)} %copy-done.55) | copy-start | bytes 1540
  566.8 129.8 %all-gather.11.cloned.1.call-start = ((), (), s32[]{:S(2)}) async-start(), calls=%async_computation.10 | async-start | bytes 5242880 | tf_op jit(solution)/shard_map/all_gather | solution.py:177
  646.7 382.4 %all-reduce.153.cloned.1.call-start = ((), (), s32[]{:S(2)}) async-start(), calls=%async_computation.12 | async-start | bytes 3145728 | tf_op jit(solution)/shard_map/psum | solution.py:284
  966.6 117.6 %reduce-scatter.11.cloned.1.call-start = ((), (), s32[]{:S(2)}) async-start(), calls=%async_computation.11 | async-start | bytes 5242880 | tf_op jit(solution)/shard_map/reduce_scatter | solution.py:206
  979.7 104.5 %copy-start.58 = (f32[128]{0:T(128)S(1)}, f32[128]{0:T(128)}, u32[]{:S(2)}) copy-start(f32[128]{0:T(128)} %copy-done.55) | copy-start | bytes 1540
  979.7 104.5 %copy-start.61 = (f32[128]{0:T(128)S(1)}, f32[128]{0:T(128)}, u32[]{:S(2)}) copy-start(f32[128]{0:T(128)} %copy-done.59) | copy-start | bytes 1540
  979.7 104.5 %copy-start.64 = (f32[128]{0:T(128)S(1)}, f32[128]{0:T(128)}, u32[]{:S(2)}) copy-start(f32[128]{0:T(128)} %copy-done.62) | copy-start | bytes 1540
  979.7 104.5 %copy-start.67 = (f32[128]{0:T(128)S(1)}, f32[128]{0:T(128)}, u32[]{:S(2)}) copy-start(f32[128]{0:T(128)} %copy-done.65) | copy-start | bytes 1540
  979.8 104.5 %copy-start.70 = (f32[128]{0:T(128)S(1)}, f32[128]{0:T(128)}, u32[]{:S(2)}) copy-start(f32[128]{0:T(128)} %copy-done.69) | copy-start | bytes 1540
  1033.2 54.0 %copy-start.92 = (f32[128]{0:T(128)S(1)}, f32[128]{0:T(128)}, u32[]{:S(2)}) copy-start(f32[128]{0:T(128)} %get-tuple-element.1298) | copy-start | bytes 1540
  1033.2 71.1 %copy-start.95 = (f32[128]{0:T(128)S(1)}, f32[128]{0:T(128)}, u32[]{:S(2)}) copy-start(f32[128]{0:T(128)} %get-tuple-element.1255) | copy-start | bytes 1540
  1033.2 72.9 %copy-start.74 = (f32[128]{0:T(128)S(1)}, f32[128]{0:T(128)}, u32[]{:S(2)}) copy-start(f32[128]{0:T(128)} %get-tuple-element.1254) | copy-start | bytes 1540
  1033.2 73.4 %copy-start.12 = (f32[2048,128]{1,0:T(8,128)S(1)}, f32[2048,128]{1,0:T(8,128)}, u32[]{:S(2)}) copy-start(f32[2048,128]{1,0:T(8,128)} %param.27) | copy-start | bytes 3145732
  1033.2 73.4 %copy-start.49 = (f32[128]{0:T(128)S(1)}, f32[128]{0:T(128)}, u32[]{:S(2)}) copy-start(f32[128]{0:T(128)} %copy-done.46) | copy-start | bytes 1540
  1033.2 73.4 %copy-start.53 = (f32[128]{0:T(128)S(1)}, f32[128]{0:T(128)}, u32[]{:S(2)}) copy-start(f32[128]{0:T(128)} %copy-done.50) | copy-start | bytes 1540
  1033.2 73.4 %copy-start.73 = (f32[128]{0:T(128)S(1)}, f32[128]{0:T(128)}, u32[]{:S(2)}) copy-start(f32[128]{0:T(128)} %get-tuple-element.1644) | copy-start | bytes 1540
  1033.2 73.4 %copy-start.91 = (f32[128]{0:T(128)S(1)}, f32[128]{0:T(128)}, u32[]{:S(2)}) copy-start(f32[128]{0:T(128)} %copy-done.90) | copy-start | bytes 1540
  1033.2 73.4 %copy-start.93 = (f32[128]{0:T(128)S(1)}, f32[128]{0:T(128)}, u32[]{:S(2)}) copy-start(f32[128]{0:T(128)} %get-tuple-element.1296) | copy-start | bytes 1540
  (58 other events, 321.2 us)
Sparse Core Ops, SparseCore 0:
  32.1 50.7 all-gather.4
  133.4 52.6 reduce-scatter.4
  208.4 49.7 all-gather.6
  365.1 52.6 reduce-scatter.6
  423.6 52.5 all-gather.8
  566.9 52.6 reduce-scatter.8
  646.8 49.7 all-gather.10
  966.7 62.3 all-reduce.152
  1032.3 51.8 reduce-scatter.10
where the time goes:
time: 1140 us; the launch traced here: 1120 us
  waiting for transfers between devices  427 us (37%)
  local copies, waits for them, and re-layouts  278 us (24%)
  other arithmetic  226 us (20%)
  matrix products  90.3 us (8%)
  blocking collectives  68.2 us (6%)
  between operations  16.6 us (1%)
    slice x336, local copies, waits for them, and re-layouts, block_scan(): summary = lax.associative_scan(compose, totals, reverse=backward, axis=1)  135 us
    reduce_scatter x2, waiting for transfers between devices, layer_backward(): lax.psum_scatter(partial_grad, 'blk', scatter_dimension=1, tiled=True)  104 us
    dynamic_update_slice x64, other arithmetic, block_scan(): lax.scan(advance, (ones_grid, zero_grid, zero_grid, zero_grid), (flag_gri...  103 us
    all_gather x2, waiting for transfers between devices, layer_forward(): normed_all = lax.all_gather(normed, 'blk', axis=1, tiled=True)  96 us
    reduce_scatter x2, waiting for transfers between devices, layer_forward(): lax.psum_scatter(partial_out, 'blk', scatter_dimension=1, tiled=True)  94.3 us
    all_gather x2, waiting for transfers between devices, layer_backward(): grad_mixed_all = lax.all_gather(grad_mixed, 'blk', axis=1, tiled=True)  84 us
    psum x1, waiting for transfers between devices, local(): lax.psum((layer_grads[0], layer_grads[1], layer_grads[2], layer_grads[3],...  49 us
    dot_general x4, matrix products, contract_rows(): lax.dot_general(matrix_left, matrix_right, (((0,), (0,)), ((), ())), prec...  38.3 us
  transfers between devices with their start and end apart: 9, of which 9 were waited for; matrix products, arithmetic and copies ran while one was open for 3% of the time, Pallas kernels for 0%

commit v1 on v0

v1 whole, which is shorter than its diff:
```python
import functools

import jax
import jax.numpy as jnp
from jax import lax
from jax.experimental import pallas as pl
from jax.experimental.pallas import tpu as pltpu
from jax.sharding import PartitionSpec as P


EPSILON = 1e-05
LANES = 128
SUBS = 8
MESH = pl.DeviceIdType.MESH
F32 = jnp.float32
BF16 = jnp.bfloat16
MATRICES = ((0, "in"), (0, "out"), (1, "in"), (1, "out"))
DIMS = {
    "nt": (((1,), (1,)), ((), ())),
    "nn": (((1,), (0,)), ((), ())),
    "tn": (((0,), (0,)), ((), ())),
}


def halves(values):
    high = values.astype(BF16)
    return high, (values - high.astype(F32)).astype(BF16)


def product(left, right, form):
    def one(a, b):
        return lax.dot_general(a, b, DIMS[form], preferred_element_type=F32)

    return one(left[0], right[0]) + (one(left[0], right[1]) + one(left[1], right[0]))


def cmul(ar, ai, br, bi):
    return ar * br - ai * bi, ar * bi + ai * br


def kernel(
    sizes,
    x_hbm,
    seq_ref,
    poles_ref,
    step_ref,
    in_hbm,
    out_mat_hbm,
    feed_ref,
    gain_ref,
    bias_ref,
    cot_hbm,
    out_hbm,
    gx_hbm,
    gpoles_ref,
    gstep_ref,
    gin_hbm,
    gout_hbm,
    gfeed_ref,
    ggain_ref,
    gbias_ref,
    xloc,
    small_src,
    small_all,
    wf,
    wh,
    wl,
    par,
    ktab,
    hid,
    cotb,
    zn,
    zh,
    zl,
    raw,
    xs,
    ybuf,
    actp,
    dyf,
    dyh,
    dyl,
    seed,
    gadj,
    dz,
    dh,
    gl,
    gsib,
    gblk,
    psum,
    gz,
    fin,
    s0_own,
    s0_sib,
    s0_z,
    s0_b,
    st_own,
    st_sib,
    st_src,
    st_buf,
    st_tot,
    cy_src,
    cy_buf,
    q_own,
    q_sib,
    q_blk,
    q_z,
    loc_s,
    sm_s,
    sm_r,
    aa_s,
    aa_r,
    w_s,
    w_r,
    wc_s,
    wc_r,
    s0c,
    s0z_s,
    s0z_r,
    s0b_s,
    s0b_r,
    stc_s,
    stc_r,
    stx_s,
    stx_r,
    cy_s,
    cy_r,
    gc_s,
    gc_r,
    gb_s,
    gb_r,
    gz_s,
    gz_r,
    ga_s,
    ga_r,
    g2_s,
    g2_r,
    qc,
    qb_s,
    qb_r,
    qz_s,
    qz_r,
):
    nb, nz, seqs, tokens, feats, states, token_count = sizes
    nch = nb * nz
    tc, fb, sb = tokens // nb, feats // nb, states // nb
    steps = tc // SUBS
    ng = states // LANES
    fl = feats // LANES
    b = lax.axis_index("blk")
    r = lax.axis_index("row")
    core = r % 2
    z = r // 2
    chip = b * nz + z
    sibling = (b, z * 2 + 1 - core)
    blk_peers = [((b + k) % nb) for k in range(1, nb)]
    z_peers = [((z + k) % nz) for k in range(1, nz)] if nz <= 8 else None

    def blk_dev(p):
        return (p, r)

    def z_dev(p):
        return (b, p * 2 + core)

    def remote(src, dst, ss, rs, dev):
        return pltpu.make_async_remote_copy(
            src, dst, ss, rs, device_id=dev, device_id_type=MESH
        )

    def over_z(body):
        if nz <= 8:
            for k in range(1, nz):
                body((z + k) % nz)
        else:

            def step(k, carry):
                body((z + k) % nz)
                return carry

            lax.fori_loop(1, nz, step, 0)

    def over_chips(body):
        def peer(k):
            q = (chip + k) % nch
            body(q, (q // nz, (q % nz) * 2 + core))

        if nch <= 16:
            for k in range(1, nch):
                peer(k)
        else:

            def step(k, carry):
                peer(k)
                return carry

            lax.fori_loop(1, nch, step, 0)

    def rows_of(i, size):
        return pl.ds(pl.multiple_of(i * size, size), size)

    my_cols = rows_of(b, fb)

    def local_copy(i, src, dst):
        return pltpu.make_async_copy(src, dst, loc_s.at[i])

    mats = [in_hbm if kind == "in" else out_mat_hbm for _, kind in MATRICES]
    locals_ = {
        "x": local_copy(0, x_hbm, xloc),
        "h": local_copy(1, x_hbm.at[rows_of(b, tc), :], hid.at[0, :, my_cols]),
        "c": local_copy(2, cot_hbm.at[rows_of(b, tc), :], cotb.at[:, my_cols]),
    }
    my_rows = pl.ds(pl.multiple_of(core * states + b * sb, 8), sb)
    for m, (layer, _) in enumerate(MATRICES):
        locals_[m] = local_copy(3 + m, mats[m].at[layer, core], wf.at[m, my_rows, :])
    for copy in locals_.values():
        copy.start()

    barrier = pltpu.get_barrier_semaphore()
    pl.semaphore_signal(barrier, 1, device_id=sibling, device_id_type=MESH)
    over_chips(
        lambda q, dev: pl.semaphore_signal(barrier, 1, device_id=dev, device_id_type=MESH)
    )

    small_src[...] = jnp.zeros_like(small_src)
    for layer in range(2):
        small_src[2 * layer : 2 * layer + 2, 0:sb] = poles_ref[layer]
    small_src[4:6, 0:sb] = step_ref[...]
    small_src[6:8, :] = feed_ref[...]
    small_src[8:10, :] = gain_ref[...]
    small_src[10:12, :] = bias_ref[...]
    small_all[b] = small_src[...]
    pl.semaphore_wait(barrier, nch)

    sends = []

    def send(copy):
        copy.start()
        sends.append(copy)

    for p in blk_peers:
        send(remote(small_src, small_all.at[b], sm_s.at[p], sm_r.at[b], blk_dev(p)))

    def send_matrix(m):
        layer = MATRICES[m][0]
        for p in blk_peers:
            send(
                remote(
                    mats[m].at[layer, core],
                    wf.at[m, my_rows, :],
                    w_s.at[m, p],
                    w_r.at[m, b],
                    blk_dev(p),
                )
            )

    def send_in(i, src, dst):
        for p in blk_peers:
            send(
                remote(
                    src.at[rows_of(p, tc), :],
                    dst.at[:, my_cols],
                    aa_s.at[i, p],
                    aa_r.at[i, b],
                    blk_dev(p),
                )
            )

    def wait_in(i, dst):
        for p in blk_peers:
            piece = dst.at[:, rows_of(p, fb)]
            remote(piece, piece, aa_s.at[i, p], aa_r.at[i, p], blk_dev(p)).wait_recv()

    def send_out(i, src, dst):
        own = pltpu.make_async_copy(
            src.at[:, my_cols], dst.at[rows_of(b, tc), :], loc_s.at[5 + i]
        )
        own.start()
        for p in blk_peers:
            send(
                remote(
                    src.at[:, rows_of(p, fb)],
                    dst.at[rows_of(b, tc), :],
                    aa_s.at[i, p],
                    aa_r.at[i, b],
                    blk_dev(p),
                )
            )
        return own

    def wait_out(i, dst):
        for p in blk_peers:
            piece = dst.at[rows_of(p, tc), :]
            remote(piece, piece, aa_s.at[i, p], aa_r.at[i, p], blk_dev(p)).wait_recv()

    def core_rows(part):
        return pl.ds(pl.multiple_of(part * states, 8), states)

    def forward_matrix(m):
        locals_[m].wait()
        for p in blk_peers:
            piece = wf.at[m, pl.ds(pl.multiple_of(core * states + p * sb, 8), sb), :]
            remote(piece, piece, w_s.at[m, p], w_r.at[m, p], blk_dev(p)).wait_recv()
        piece = wf.at[m, core_rows(core), :]
        send(remote(piece, piece, wc_s.at[m], wc_r.at[m], sibling))

    def split_matrix(m):
        piece = wf.at[m, core_rows(1 - core), :]
        remote(piece, piece, wc_s.at[m], wc_r.at[m], sibling).wait_recv()
        scaled = MATRICES[m][1] == "out"
        for part in range(2):

            def body(i, carry, part=part):
                rows = pl.ds(pl.multiple_of(part * states + i * 64, 64), 64)
                values = wf[m, rows, :]
                if scaled:
                    values = values * (2.0 - 4.0 * part)
                wh[m, rows, :], wl[m, rows, :] = halves(values)
                return carry

            lax.fori_loop(0, states // 64, body, 0)

    send_matrix(0)
    locals_["x"].wait()

    def add_rows(i, carry):
        total, square = carry
        values = xloc[rows_of(i, 64), :].reshape(8, SUBS, LANES * (fb // LANES))
        return total + jnp.sum(values, axis=0), square + jnp.sum(values * values, axis=0)

    zero_tile = jnp.zeros((SUBS, fb), F32)
    total, square = lax.fori_loop(0, tokens // 64, add_rows, (zero_tile, zero_tile))
    s0_own[...] = jnp.zeros_like(s0_own)
    s0_own[0:1, :] = jnp.sum(total, axis=0, keepdims=True)
    s0_own[1:2, :] = jnp.sum(square, axis=0, keepdims=True)
    copy = remote(s0_own, s0_sib, s0c.at[0], s0c.at[1], sibling)
    copy.start()
    copy.wait_recv()
    s0_z[z] = s0_own[...] + s0_sib[...]
    sends.append(copy)
    over_z(
        lambda p: remote(
            s0_z.at[z], s0_z.at[z], s0z_s.at[p], s0z_r.at[z], z_dev(p)
        ).start()
    )
    over_z(
        lambda p: remote(
            s0_z.at[p], s0_z.at[p], s0z_s.at[p], s0z_r.at[p], z_dev(p)
        ).wait()
    )
    s0_b[b] = jnp.sum(s0_z[...], axis=0)
    for p in blk_peers:
        send(remote(s0_b.at[b], s0_b.at[b], s0b_s.at[p], s0b_r.at[b], blk_dev(p)))
    send_in(0, x_hbm, hid.at[0])
    send_matrix(1)

    for p in blk_peers:
        remote(
            small_all.at[p], small_all.at[p], sm_s.at[p], sm_r.at[p], blk_dev(p)
        ).wait_recv()
    state_rows = jnp.concatenate([small_all[p][0:8, 0:sb] for p in range(nb)], axis=1)

    def feature_row(row):
        return jnp.concatenate([small_all[p][row : row + 1, :] for p in range(nb)], axis=1)

    def discretize(real, imag, log_step):
        step = jnp.exp(log_step)
        magnitude = jnp.exp(real * step)
        lr = magnitude * jnp.cos(imag * step)
        li = magnitude * jnp.sin(imag * step)
        modulus = real * real + imag * imag
        fr = ((lr - 1.0) * real + li * imag) / modulus
        fi = (li * real - (lr - 1.0) * imag) / modulus
        return step, lr, li, fr, fi, modulus

    for layer in range(2):
        _, lr, li, fr, fi, _ = discretize(
            state_rows[2 * layer : 2 * layer + 1, :],
            state_rows[2 * layer + 1 : 2 * layer + 2, :],
            state_rows[4 + layer : 5 + layer, :],
        )
        power = [(lr, li)]
        size = 1
        while size < tc:
            power.append(cmul(*power[-1], *power[-1]))
            size *= 2
        at_steps = power[steps.bit_length() - 1]
        for row, value in enumerate((lr, li, fr, fi, *at_steps, *power[-1])):
            par[layer, row : row + 1, :] = value

    def wide(layer, row, group):
        part = par[layer, row : row + 1, group * LANES : (group + 1) * LANES]
        return jnp.broadcast_to(part, (SUBS, LANES))

    starts = [jnp.int32(0)]
    for i in range(seqs - 1):
        starts.append(starts[-1] + seq_ref[0, i])
    begins = starts
    ends = starts[1:] + [jnp.int32(tokens)]

    def none_in(low, size, marks, shift):
        hit = None
        for mark in marks:
            at = mark - shift - low
            inside = jnp.logical_and(at >= 0, at < size)
            hit = inside if hit is None else jnp.logical_or(hit, inside)
        return jnp.where(hit, 0.0, 1.0).astype(F32)

    sub_index = lax.broadcasted_iota(jnp.int32, (SUBS, LANES), 0)
    base = b * tc
    marks = ((begins, 0), (ends, 1))

    def fill_flags(k, carry):
        for way in range(2):
            ktab[way, k] = none_in(base + sub_index * steps + k, 1, *marks[way])
        return carry

    lax.fori_loop(0, steps, fill_flags, 0)
    whole_sub = [none_in(base + sub_index * steps, steps, *marks[way]) for way in range(2)]
    whole_chunk = [[none_in(p * tc, tc, *marks[way]) for p in range(nb)] for way in range(2)]

    def load(ref, g, k):
        return ref[g, pl.ds(k, SUBS, stride=steps), :]

    def recur(carry, keep, lam, pushes):
        gated = [c * keep for c in carry]
        new = []
        for g in range(ng):
            vr, vi = cmul(lam[0][g], lam[1][g], gated[g], gated[ng + g])
            new.append((vr + pushes[g], vi + pushes[ng + g]))
        return gated, [v[0] for v in new] + [v[1] for v in new]

    def scan_local(src, lam, way, reverse):
        def body(i, carry):
            k = steps - 1 - i if reverse else i
            pushes = [load(src, g, k) for g in range(2 * ng)]
            return tuple(recur(carry, ktab[way, k], lam, pushes)[1])

        zero = jnp.zeros((SUBS, LANES), F32)
        return lax.fori_loop(0, steps, body, (zero,) * (2 * ng), unroll=4)

    def prefix(last, power, way, reverse):
        out = []
        for g in range(ng):
            sr, si = last[g], last[ng + g]
            ar, ai = power[0][g] * whole_sub[way], power[1][g] * whole_sub[way]
            for d in (1, 2, 4):
                shift = SUBS - d if reverse else d
                ok = sub_index < SUBS - d if reverse else sub_index >= d
                tr, ti = cmul(ar, ai, pltpu.roll(sr, shift, 0), pltpu.roll(si, shift, 0))
                br, bi = cmul(ar, ai, pltpu.roll(ar, shift, 0), pltpu.roll(ai, shift, 0))
                sr, si = jnp.where(ok, sr + tr, sr), jnp.where(ok, si + ti, si)
                ar, ai = jnp.where(ok, br, ar), jnp.where(ok, bi, ai)
            out.append((sr, si, ar, ai))
        return out

    def send_carry(e, pre, reverse):
        row = 0 if reverse else SUBS - 1
        for g in range(ng):
            cols = slice(g * LANES, (g + 1) * LANES)
            for part in range(2):
                cy_src[e, part : part + 1, cols] = pre[g][part][row : row + 1, :]
                cy_buf[e, b, part : part + 1, cols] = pre[g][part][row : row + 1, :]
        for p in blk_peers:
            send(
                remote(cy_src.at[e], cy_buf.at[e, b], cy_s.at[e, p], cy_r.at[e, b], blk_dev(p))
            )

    def take_carry(e, pre, layer, way, reverse, sign):
        for p in blk_peers:
            piece = cy_buf.at[e, p]
            remote(cy_src.at[e], piece, cy_s.at[e, p], cy_r.at[e, p], blk_dev(p)).wait_recv()
        ar, ai = par[layer, 6:7, :], sign * par[layer, 7:8, :]
        zero = jnp.zeros((1, states), F32)
        cr, ci, er, ei = zero, zero, zero, zero
        for p in reversed(range(nb)) if reverse else range(nb):
            er, ei = jnp.where(b == p, cr, er), jnp.where(b == p, ci, ei)
            tr, ti = cmul(ar, ai, cr, ci)
            keep = whole_chunk[way][p]
            cr = cy_buf[e, p, 0:1, :] + keep * tr
            ci = cy_buf[e, p, 1:2, :] + keep * ti
        shift = SUBS - 1 if reverse else 1
        first = sub_index == (SUBS - 1 if reverse else 0)
        carry_r, carry_i = [], []
        for g in range(ng):
            cols = slice(g * LANES, (g + 1) * LANES)
            wr = jnp.broadcast_to(er[:, cols], (SUBS, LANES))
            wi = jnp.broadcast_to(ei[:, cols], (SUBS, LANES))
            sr, si, dr, di = (pltpu.roll(v, shift, 0) for v in pre[g])
            tr, ti = cmul(dr, di, wr, wi)
            carry_r.append(jnp.where(first, wr, sr + tr))
            carry_i.append(jnp.where(first, wi, si + ti))
        return tuple(carry_r + carry_i)

    def forward_states(layer, carry, way, reverse, lam):
        scale = [[wide(layer, 2 + part, g) for g in range(ng)] for part in range(2)]
        src, dst = raw.at[layer], xs.at[layer]

        def body(i, carry):
            k = steps - 1 - i if reverse else i
            pushes = [load(src, g, k) for g in range(2 * ng)]
            _, new = recur(carry, ktab[way, k], lam, pushes)
            for g in range(ng):
                vr, vi = cmul(scale[0][g], scale[1][g], new[g], new[ng + g])
                dst[g, pl.ds(k, SUBS, stride=steps), :] = vr
                dst[ng + g, pl.ds(k, SUBS, stride=steps), :] = vi
            return tuple(new)

        lax.fori_loop(0, steps, body, carry, unroll=2)

    def adjoint_states(layer, carry, way, reverse, lam):
        scale = [[wide(layer, 2 + part, g) for g in range(ng)] for part in range(2)]
        zero = jnp.zeros((SUBS, LANES), F32)

        def body(i, loop):
            carry, sums = loop
            k = steps - 1 - i if reverse else i
            at = pl.ds(k, SUBS, stride=steps)
            pushes = [load(seed, g, k) for g in range(2 * ng)]
            gated, new = recur(carry, ktab[way, k], lam, pushes)
            sums = list(sums)
            for g in range(ng):
                xr, xi = xs[layer, g, at, :], xs[layer, ng + g, at, :]
                ur, ui = raw[layer, g, at, :], raw[layer, ng + g, at, :]
                pr, pi = gated[g], gated[ng + g]
                vr, vi = new[g], new[ng + g]
                sums[g] += pr * xr + pi * xi
                sums[ng + g] += pi * xr - pr * xi
                sums[2 * ng + g] += vr * ur + vi * ui
                sums[3 * ng + g] += vi * ur - vr * ui
                gadj[g, at, :] = scale[0][g] * vr + scale[1][g] * vi
                gadj[ng + g, at, :] = scale[0][g] * vi - scale[1][g] * vr
            return tuple(new), tuple(sums)

        return lax.fori_loop(0, steps, body, (carry, (zero,) * (4 * ng)))[1]

    tile = 256 if tc % 256 == 0 else tc

    def to_groups(left, m, dst):
        def body(i, carry):
            rows = rows_of(i, tile)
            value = product(
                (left[0][rows, :], left[1][rows, :]), (wh[m], wl[m]), "nt"
            )
            for g in range(2 * ng):
                dst[g, rows, :] = value[:, g * LANES : (g + 1) * LANES]
            return carry

        lax.fori_loop(0, tc // tile, body, 0)

    def from_groups(src, m, dst):
        def body(i, carry):
            rows = rows_of(i, tile)
            left = jnp.concatenate([src[g, rows, :] for g in range(2 * ng)], axis=1)
            dst[rows, :] = product(halves(left), (wh[m], wl[m]), "nn")
            return carry

        lax.fori_loop(0, tc // tile, body, 0)

    def weight_grad(src, right, m, scaled):
        def body(pair, carry):
            left = jnp.concatenate([src[2 * pair], src[2 * pair + 1]], axis=1)
            value = product(halves(left), (right[0][...], right[1][...]), "tn")
            for half in range(2):
                g = 2 * pair + half
                part = value[half * LANES : (half + 1) * LANES, :]
                if scaled:
                    part = part * jnp.where(g < ng, 2.0, -2.0)
                gl[m, rows_of(g, LANES), :] = part
            return carry

        lax.fori_loop(0, ng, body, 0)

    def stats_start(i, first, second):
        for n, value in enumerate((first, second)):
            for j in range(fl):
                row = n * fl + j
                st_own[i, row : row + 1, :] = value[:, j * LANES : (j + 1) * LANES]
        copy = remote(st_own.at[i], st_sib.at[i], stc_s.at[i], stc_r.at[i], sibling)
        send(copy)
        copy.wait_recv()
        both = st_own[i] + st_sib[i]
        st_src[i] = both
        st_buf[i, chip] = both
        over_chips(
            lambda q, dev: remote(
                st_src.at[i], st_buf.at[i, chip], stx_s.at[i, q], stx_r.at[i, chip], dev
            ).start()
        )

    def stats_end(i):
        over_chips(
            lambda q, dev: remote(
                st_src.at[i], st_buf.at[i, q], stx_s.at[i, q], stx_r.at[i, q], dev
            ).wait()
        )
        st_tot[i] = jnp.sum(st_buf[i], axis=0)
        return [
            jnp.concatenate(
                [st_tot[i, n * fl + j : n * fl + j + 1, :] for j in range(fl)], axis=1
            )
            for n in range(2)
        ]

    def to_row(value):
        return jnp.sum(value, axis=0, keepdims=True)

    def eights(value):
        return jnp.sum(value.reshape(value.shape[0] // SUBS, SUBS, feats), axis=0)

    def grad_core(m):
        send(
            remote(gl.at[m, core_rows(1 - core), :], gsib.at[m], gc_s.at[m], gc_r.at[m], sibling)
        )

    def grad_blk(m):
        remote(gsib.at[m], gsib.at[m], gc_s.at[m], gc_r.at[m], sibling).wait_recv()

        def body(i, carry):
            rows = rows_of(i, 32)
            own = pl.ds(pl.multiple_of(core * states + i * 32, 32), 32)
            gsib[m, rows, :] += gl[m, own, :]
            return carry

        lax.fori_loop(0, states // 32, body, 0)
        for p in blk_peers:
            piece = gsib.at[m, pl.ds(pl.multiple_of(p * sb, 8), sb), :]
            send(remote(piece, gblk.at[m, b], gb_s.at[m, p], gb_r.at[m, b], blk_dev(p)))

    pr = psum.shape[1] // nz

    def grad_z(m):
        for p in blk_peers:
            piece = gblk.at[m, p]
            remote(piece, piece, gb_s.at[m, p], gb_r.at[m, p], blk_dev(p)).wait_recv()
        own = pl.ds(pl.multiple_of(b * sb, 8), sb)
        for j in range(fl):
            cols = slice(j * LANES, (j + 1) * LANES)
            value = gsib[m, own, cols]
            for p in blk_peers:
                value += gblk[m, p, :, cols]
            psum[m, j * sb : (j + 1) * sb, :] = value
        over_z(
            lambda p: remote(
                psum.at[m, rows_of(p, pr), :], gz.at[m, z], gz_s.at[m, p], gz_r.at[m, z], z_dev(p)
            ).start()
        )

    def grad_gather(m):
        over_z(
            lambda p: remote(
                psum.at[m, rows_of(p, pr), :], gz.at[m, p], gz_s.at[m, p], gz_r.at[m, p], z_dev(p)
            ).wait()
        )
        mine = rows_of(z, pr)
        gz[m, z] = psum[m, mine, :]
        value = gz[m, 0]
        for p in range(1, nz):
            value += gz[m, p]
        fin[m, core, mine, :] = value
        piece = fin.at[m, core, mine, :]
        over_z(
            lambda p: remote(piece, piece, ga_s.at[m, p], ga_r.at[m, z], z_dev(p)).start()
        )

    def grad_share(m):
        def arrive(p):
            piece = fin.at[m, core, rows_of(p, pr), :]
            remote(piece, piece, ga_s.at[m, p], ga_r.at[m, p], z_dev(p)).wait()

        over_z(arrive)
        piece = fin.at[m, core]
        send(remote(piece, piece, g2_s.at[m], g2_r.at[m], sibling))

    stores = []

    def grad_store(m):
        piece = fin.at[m, 1 - core]
        remote(piece, piece, g2_s.at[m], g2_r.at[m], sibling).wait_recv()
        layer, kind = MATRICES[m]
        dst = gin_hbm if kind == "in" else gout_hbm
        for part in range(2):
            for j in range(fl):
                copy = pltpu.make_async_copy(
                    fin.at[m, part, j * sb : (j + 1) * sb, :],
                    dst.at[layer, part, :, j * LANES : (j + 1) * LANES],
                    loc_s.at[9 + (m * 2 + part) * fl + j],
                )
                copy.start()
                stores.append(copy)

    for p in blk_peers:
        remote(s0_b.at[p], s0_b.at[p], s0b_s.at[p], s0b_r.at[p], blk_dev(p)).wait_recv()
    sums = [
        jnp.concatenate([s0_b[p][n : n + 1, :] for p in range(nb)], axis=1) for n in range(2)
    ]
    forward_matrix(0)
    split_matrix(0)
    locals_["h"].wait()
    wait_in(0, hid.at[0])

    scales = []
    small_rows = 32

    for layer in range(2):
        way, reverse = layer, layer == 1
        mean = sums[0] / token_count
        rstd = lax.rsqrt(sums[1] / token_count - mean * mean + EPSILON)
        gain, bias, feed = (feature_row(row + layer) for row in (8, 10, 6))
        scales.append((rstd, gain, bias, feed))

        def normalize(i, carry, layer=layer, mean=mean, rstd=rstd, gain=gain, bias=bias):
            rows = rows_of(i, small_rows)
            unit = (hid[layer, rows, :] - mean) * rstd
            zn[layer, rows, :] = unit
            zh[layer, rows, :], zl[layer, rows, :] = halves(gain * unit + bias)
            return carry

        lax.fori_loop(0, tc // small_rows, normalize, 0)
        to_groups((zh.at[layer], zl.at[layer]), 2 * layer, raw.at[layer])
        lam = [[wide(layer, part, g) for g in range(ng)] for part in range(2)]
        power = [[wide(layer, 4 + part, g) for g in range(ng)] for part in range(2)]
        last = scan_local(raw.at[layer], lam, way, reverse)
        pre = prefix(last, power, way, reverse)
        send_carry(layer, pre, reverse)
        if layer == 0:
            send_matrix(2)
        forward_matrix(2 * layer + 1)
        split_matrix(2 * layer + 1)
        carry = take_carry(layer, pre, layer, way, reverse, 1.0)
        forward_states(layer, carry, way, reverse, lam)
        from_groups(xs.at[layer], 2 * layer + 1, ybuf)

        def activate(i, carry, layer=layer, gain=gain, bias=bias, feed=feed):
            rows = rows_of(i, small_rows)
            mixed = ybuf[rows, :] + feed * (gain * zn[layer, rows, :] + bias)
            below = 0.5 * (1.0 + lax.erf(mixed * 0.7071067811865476))
            density = 0.3989422804014327 * jnp.exp(-0.5 * mixed * mixed)
            gate = 1.0 / (1.0 + jnp.exp(-mixed))
            gelu = mixed * below
            value = hid[layer, rows, :] + gelu * gate
            hid[layer + 1, rows, :] = value
            actp[layer, rows, :] = (below + mixed * density) * gate + gelu * gate * (1.0 - gate)
            return carry[0] + eights(value), carry[1] + eights(value * value)

        zero = jnp.zeros((SUBS, feats), F32)
        parts = lax.fori_loop(0, tc // small_rows, activate, (zero, zero))
        if layer == 0:
            stats_start(0, to_row(parts[0]), to_row(parts[1]))
            send_matrix(3)
            send_in(1, cot_hbm, cotb)
            forward_matrix(2)
            split_matrix(2)
            sums = stats_end(0)

    own_out = send_out(2, hid.at[2], out_hbm)
    locals_["c"].wait()
    wait_in(1, cotb)
    totals = {}
    for layer in (1, 0):
        way, reverse = 1 - layer, layer == 0
        rstd, gain, bias, feed = scales[layer]
        upper = cotb if layer == 1 else dh.at[0]

        def mixed_grad(i, carry, layer=layer, gain=gain, bias=bias, upper=upper):
            rows = rows_of(i, small_rows)
            value = upper[rows, :] * actp[layer, rows, :]
            dyf[rows, :] = value
            dyh[rows, :], dyl[rows, :] = halves(value)
            return carry + eights(value * (gain * zn[layer, rows, :] + bias))

        zero = jnp.zeros((SUBS, feats), F32)
        feed_grad = to_row(lax.fori_loop(0, tc // small_rows, mixed_grad, zero))
        to_groups((dyh, dyl), 2 * layer + 1, seed)
        lam = [
            [wide(layer, 0, g) for g in range(ng)],
            [-wide(layer, 1, g) for g in range(ng)],
        ]
        power = [
            [wide(layer, 4, g) for g in range(ng)],
            [-wide(layer, 5, g) for g in range(ng)],
        ]
        last = scan_local(seed, lam, way, reverse)
        pre = prefix(last, power, way, reverse)
        send_carry(2 + layer, pre, reverse)
        weight_grad(xs.at[layer], (dyh, dyl), 2 * layer + 1, True)
        grad_core(2 * layer + 1)
        carry = take_carry(2 + layer, pre, layer, way, reverse, -1.0)
        state_sums = adjoint_states(layer, carry, way, reverse, lam)
        grad_blk(2 * layer + 1)
        from_groups(gadj, 2 * layer, dz)

        def dz_sums(i, carry, layer=layer, feed=feed):
            rows = rows_of(i, small_rows)
            value = dz[rows, :] + feed * dyf[rows, :]
            dz[rows, :] = value
            return carry[0] + eights(value), carry[1] + eights(value * zn[layer, rows, :])

        parts = lax.fori_loop(0, tc // small_rows, dz_sums, (zero, zero))
        stats_start(1 + layer, to_row(parts[0]), to_row(parts[1]))
        weight_grad(gadj, (zh.at[layer], zl.at[layer]), 2 * layer, False)
        grad_core(2 * layer)
        for p in range(nb):
            q_own[p, layer : layer + 1, :] = feed_grad[:, p * fb : (p + 1) * fb]
        for n in range(4):
            vector = jnp.concatenate(
                [to_row(state_sums[n * ng + g]) for g in range(ng)], axis=1
            )
            row = 2 + 4 * layer + n
            for p in range(nb):
                q_own[p, row : row + 1, 0:sb] = vector[:, p * sb : (p + 1) * sb]
        grad_blk(2 * layer)
        grad_z(2 * layer + 1)
        bias_grad, gain_grad = stats_end(1 + layer)

        def hidden_grad(i, carry, layer=layer, rstd=rstd, gain=gain, bias_grad=bias_grad, gain_grad=gain_grad, upper=upper):
            rows = rows_of(i, small_rows)
            inner = (
                dz[rows, :]
                - bias_grad / token_count
                - zn[layer, rows, :] * (gain_grad / token_count)
            )
            dh[1 - layer, rows, :] = upper[rows, :] + gain * rstd * inner
            return carry

        lax.fori_loop(0, tc // small_rows, hidden_grad, 0)
        ggain_ref[layer : layer + 1, :] = st_tot[1 + layer, pl.ds(fl + b, 1), :]
        gbias_ref[layer : layer + 1, :] = st_tot[1 + layer, pl.ds(b, 1), :]
        if layer == 1:
            grad_gather(3)
            grad_z(2)

    own_gx = send_out(3, dh.at[1], gx_hbm)

    copy = remote(q_own, q_sib, qc.at[0], qc.at[1], sibling)
    send(copy)
    grad_share(3)
    grad_gather(2)
    copy.wait_recv()
    q_sib[...] += q_own[...]
    for p in blk_peers:
        send(remote(q_sib.at[p], q_blk.at[b], qb_s.at[p], qb_r.at[b], blk_dev(p)))
    grad_store(3)
    grad_gather(1)
    grad_share(2)
    grad_z(0)
    grad_store(2)
    grad_share(1)
    for p in blk_peers:
        remote(q_blk.at[p], q_blk.at[p], qb_s.at[p], qb_r.at[p], blk_dev(p)).wait_recv()
    value = q_sib[b]
    for p in blk_peers:
        value += q_blk[p]
    q_z[z] = value
    over_z(
        lambda p: remote(q_z.at[z], q_z.at[z], qz_s.at[p], qz_r.at[z], z_dev(p)).start()
    )
    grad_gather(0)
    grad_store(1)
    over_z(
        lambda p: remote(q_z.at[p], q_z.at[p], qz_s.at[p], qz_r.at[p], z_dev(p)).wait()
    )
    small = jnp.sum(q_z[...], axis=0)
    gfeed_ref[...] = small[0:2, :]
    for layer in range(2):
        real = poles_ref[layer, 0:1, :]
        imag = poles_ref[layer, 1:2, :]
        step, lr, li, fr, fi, modulus = discretize(real, imag, step_ref[layer : layer + 1, :])
        lgr, lgi, fgr, fgi = (
            small[2 + 4 * layer + n : 3 + 4 * layer + n, 0:sb] for n in range(4)
        )
        qr = (real * fgr - imag * fgi) / modulus
        qi = (real * fgi + imag * fgr) / modulus
        tr, ti = lgr + qr, lgi + qi
        wr = lr * tr + li * ti
        wi = lr * ti - li * tr
        gpoles_ref[layer, 0:1, :] = step * wr - (fr * qr + fi * qi)
        gpoles_ref[layer, 1:2, :] = step * wi - (fr * qi - fi * qr)
        gstep_ref[layer : layer + 1, :] = step * (real * wr + imag * wi)
    grad_share(0)
    grad_store(0)
    wait_out(2, out_hbm)
    wait_out(3, gx_hbm)
    own_out.wait()
    own_gx.wait()
    for copy in stores:
        copy.wait()
    for copy in sends:
        copy.wait_send()


def local(mesh, *args):
    inputs, seq_lengths = args[0], args[1]
    nb, nr = mesh.shape["blk"], mesh.shape["row"]
    nz = nr // 2
    tokens, fb = inputs.shape
    sb = args[2].shape[2]
    states, feats = sb * nb, fb * nb
    assert seq_lengths.shape[0] == 1 and nr % 2 == 0
    assert fb % LANES == 0 and states % LANES == 0 and 2 * feats == SUBS * LANES
    assert tokens % (nb * SUBS * SUBS) == 0
    tc = tokens // nb
    steps = tc // SUBS
    assert steps & (steps - 1) == 0
    nch = nb * nz
    fl = feats // LANES
    ng2 = 2 * states // LANES
    piece = -(-fl * sb // (nz * SUBS)) * SUBS
    sizes = (nb, nz, seq_lengths.shape[1], tokens, feats, states, tokens * nr)
    vmem = lambda *shape: pltpu.VMEM(shape, F32)
    half = lambda *shape: pltpu.VMEM(shape, BF16)
    dma = lambda *shape: pltpu.SemaphoreType.DMA(shape)
    scratch = [
        vmem(tokens, fb),
        vmem(16, fb),
        vmem(nb, 16, fb),
        vmem(4, 2 * states, feats),
        half(4, 2 * states, feats),
        half(4, 2 * states, feats),
        vmem(2, 8, states),
        vmem(2, steps, SUBS, LANES),
        vmem(3, tc, feats),
        vmem(tc, feats),
        vmem(2, tc, feats),
        half(2, tc, feats),
        half(2, tc, feats),
        vmem(2, ng2, tc, LANES),
        vmem(2, ng2, tc, LANES),
        vmem(tc, feats),
        vmem(2, tc, feats),
        vmem(tc, feats),
        half(tc, feats),
        half(tc, feats),
        vmem(ng2, tc, LANES),
        vmem(ng2, tc, LANES),
        vmem(tc, feats),
        vmem(2, tc, feats),
        vmem(4, 2 * states, feats),
        vmem(4, states, feats),
        vmem(4, nb, sb, feats),
        vmem(4, nz * piece, LANES),
        vmem(4, nz, piece, LANES),
        vmem(4, 2, nz * piece, LANES),
        vmem(8, fb),
        vmem(8, fb),
        vmem(nz, 8, fb),
        vmem(nb, 8, fb),
        vmem(3, 8, LANES),
        vmem(3, 8, LANES),
        vmem(3, 8, LANES),
        vmem(3, nch, 8, LANES),
        vmem(3, 8, LANES),
        vmem(4, 8, states),
        vmem(4, nb, 8, states),
        vmem(nb, 16, fb),
        vmem(nb, 16, fb),
        vmem(nb, 16, fb),
        vmem(nz, 16, fb),
        dma(9 + 8 * fl),
        dma(nb),
        dma(nb),
        dma(4, nb),
        dma(4, nb),
        dma(4, nb),
        dma(4, nb),
        dma(4),
        dma(4),
        dma(2),
        dma(nz),
        dma(nz),
        dma(nb),
        dma(nb),
        dma(3),
        dma(3),
        dma(3, nch),
        dma(3, nch),
        dma(4, nb),
        dma(4, nb),
        dma(4),
        dma(4),
        dma(4, nb),
        dma(4, nb),
        dma(4, nz),
        dma(4, nz),
        dma(4, nz),
        dma(4, nz),
        dma(4),
        dma(4),
        dma(2),
        dma(nb),
        dma(nb),
        dma(nz),
        dma(nz),
    ]
    shaped = lambda like: jax.ShapeDtypeStruct(like.shape, like.dtype)
    anywhere = pl.BlockSpec(memory_space=pl.ANY)
    fast = pl.BlockSpec(memory_space=pltpu.VMEM)
    return pl.pallas_call(
        functools.partial(kernel, sizes),
        name="s5_layers",
        out_shape=tuple(shaped(args[i]) for i in (0, 0, 2, 3, 4, 5, 6, 7, 8)),
        in_specs=[
            anywhere,
            pl.BlockSpec(memory_space=pltpu.SMEM),
            fast,
            fast,
            anywhere,
            anywhere,
            fast,
            fast,
            fast,
            anywhere,
        ],
        out_specs=(anywhere, anywhere, fast, fast, anywhere, anywhere, fast, fast, fast),
        scratch_shapes=scratch,
        compiler_params=pltpu.CompilerParams(
            collective_id=0, has_side_effects=True, vmem_limit_bytes=60 << 20
        ),
    )(*args)


def solution(mesh):
    by_state = (P(None, None, "blk"), P(None, "blk"), P(None, None, "blk", None), P(None, None, "blk", None))
    by_feature = (P(None, "blk"),) * 3
    tokens = P("row", "blk")
    return jax.shard_map(
        functools.partial(local, mesh),
        mesh=mesh,
        in_specs=(tokens, P("row", None), *by_state, *by_feature, tokens),
        out_specs=(tokens, tokens, *by_state, *by_feature),
        check_vma=False,
    )
```

time: 1140 us -> 182 us (0.16); the launches traced: 1120 us -> 180 us
  waiting for transfers between devices: 427 us -> 0 us
  local copies, waits for them, and re-layouts: 278 us -> 8.66 us
  other arithmetic: 226 us -> 0 us
  Pallas kernels: 0 us -> 171 us
  matrix products: 90.3 us -> 0 us
  blocking collectives: 68.2 us -> 0 us
  between operations: 16.6 us -> 0.67 us
    reduce_scatter x4 -> x0, waiting for transfers between devices: 198 us -> none  [the longest x2 104 us: layer_backward(): lax.psum_scatter(partial_grad, 'blk', scatter_dimension=1, tiled=True)]
    all_gather x4 -> x0, waiting for transfers between devices: 180 us -> none  [the longest x2 96 us: layer_forward(): normed_all = lax.all_gather(normed, 'blk', axis=1, tiled=True)]
    pallas_call x0 -> x1, Pallas kernels: none -> 171 us  [local(): pl.pallas_call(functools.partial(kernel, sizes), name='s5_layers', out_sh...]
    slice x361 -> x0, local copies, waits for them, and re-layouts: 159 us -> none  [the longest x336 135 us: block_scan(): summary = lax.associative_scan(compose, totals, reverse=backward, axis=1)]
    dynamic_update_slice x64 -> x0, other arithmetic: 103 us -> none  [block_scan(): lax.scan(advance, (ones_grid, zero_grid, zero_grid, zero_grid), (flag_gri...]
    dot_general x12 -> x0, matrix products: 90.3 us -> none  [the longest x4 38.3 us: contract_rows(): lax.dot_general(matrix_left, matrix_right, (((0,), (0,)), ((), ())), prec...]
    psum x4 -> x0, blocking collectives: 68.2 us -> none  [the longest x2 34.6 us: layer_forward(): lax.psum((jnp.sum(hidden, axis=0), jnp.sum(hidden * hidden, axis=0)), 'row')]
    psum x1 -> x0, waiting for transfers between devices: 49 us -> none  [local(): lax.psum((layer_grads[0], layer_grads[1], layer_grads[2], layer_grads[3],...]
  transfers between devices with their start and end apart: 9 -> 0, of which waited for: 9 -> 0; matrix products, arithmetic and copies ran while one was open for 3% -> 0% of each run, Pallas kernels for 0% -> 0%
where the time goes in v1:
time: 182 us; the launch traced here: 180 us
  Pallas kernels  171 us (94%)
  local copies, waits for them, and re-layouts  8.66 us (5%)
    pallas_call x1, Pallas kernels, local(): pl.pallas_call(functools.partial(kernel, sizes), name='s5_layers', out_sh...  171 us
    unnamed x25, local copies, waits for them, and re-layouts  8.66 us

profile of v1, /device:TPU:0, one launch (start us, length us, event | category | flops | bytes accessed | tf_op | source)
XLA Modules:
  0.0 180.4 jit_solution(3048093462572160890)
XLA Ops:
  0.6 171.1 %s5_layers.1 = (f32[2048,128]{1,0:T(8,128)}, f32[2048,128]{1,0:T(8,128)}, f32[2,2,96]{2,1,0:T(2,128)}, f32[2,96]{1,0:T(2,128)}, f32[2,2,96,512]{3,2,1,0:T(8,128)...) custom-call(f32[2048,128]{1,0:T(8,128)} %x_hbm.1, s32[1,3]{1,0:T(1,128)} %seq_ref.1, ...), custom_call_target="tpu_custom_call" | custom-call | tf_op jit(solution)/shard_map/s5_layers/pallas_call | solution.py:996
  171.8 0.0 copy-start
  171.8 2.4 %copy.28 = f32[2048,128]{1,0:T(8,128)} copy(f32[2048,128]{1,0:T(8,128)} %get-tuple-element.18) | data formatting | bytes 2097152
  174.1 0.0 copy-done
  174.1 0.0 copy-start.3
  174.1 0.0 copy-start.2
  174.1 1.0 copy.29
  175.1 0.0 copy-done.3
  175.1 0.0 copy-start.7
  175.1 0.6 copy.30
  175.7 0.1 copy-done.7
  175.8 0.6 copy.31
  176.3 0.0 copy-done.2
  176.3 0.0 copy-start.1
  176.3 0.9 copy.32
  177.2 0.5 copy-done.1
  177.8 0.0 copy-start.6
  177.8 0.9 copy.33
  178.6 0.0 copy-done.6
  178.6 0.0 copy-start.5
  178.6 0.6 copy.34
  179.2 0.1 copy-done.5
  179.3 0.0 copy-start.4
  179.3 0.6 copy.35
  179.8 0.0 copy-done.4
  179.9 0.6 copy.36
Async XLA Ops:
  171.8 2.4 %copy-start = (f32[2048,128]{1,0:T(8,128)S(1)}, f32[2048,128]{1,0:T(8,128)}, u32[]{:S(2)}) copy-start(f32[2048,128]{1,0:T(8,128)} %get-tuple-element.19) | copy-start | bytes 3145732
  174.1 1.0 copy-start.3
  174.1 2.2 %copy-start.2 = (f32[2,2,96,512]{3,2,1,0:T(8,128)S(1)}, f32[2,2,96,512]{3,2,1,0:T(8,128)}, u32[]{:S(2)}) copy-start(f32[2,2,96,512]{3,2,1,0:T(8,128)} %get-tuple-element.22) | copy-start | bytes 2359300
  175.1 0.7 copy-start.7
  176.3 1.4 copy-start.1
  177.8 0.9 copy-start.6
  178.6 0.6 copy-start.5
  179.3 0.6 copy-start.4

commit v2 on v1

v2 whole, which is shorter than its diff:
```python
import functools

import jax
import jax.numpy as jnp
from jax import lax
from jax.experimental import pallas as pl
from jax.experimental.pallas import tpu as pltpu
from jax.sharding import PartitionSpec as P


EPSILON = 1e-05
LANES = 128
SUBS = 8
MESH = pl.DeviceIdType.MESH
F32 = jnp.float32
BF16 = jnp.bfloat16
MATRICES = ((0, "in"), (0, "out"), (1, "in"), (1, "out"))
SHARED = (True, False, True, True)
SEMAPHORES = 128
DIMS = {
    "nt": (((1,), (1,)), ((), ())),
    "nn": (((1,), (0,)), ((), ())),
    "tn": (((0,), (0,)), ((), ())),
}


def halves(values):
    high = values.astype(BF16)
    return high, (values - high.astype(F32)).astype(BF16)


def product(left, right, form):
    def one(a, b):
        return lax.dot_general(a, b, DIMS[form], preferred_element_type=F32)

    return one(left[0], right[0]) + (one(left[0], right[1]) + one(left[1], right[0]))


def cmul(ar, ai, br, bi):
    return ar * br - ai * bi, ar * bi + ai * br


def kernel(
    sizes,
    x_hbm,
    seq_ref,
    poles_ref,
    step_ref,
    in_hbm,
    out_mat_hbm,
    feed_ref,
    gain_ref,
    bias_ref,
    cot_hbm,
    out_hbm,
    gx_hbm,
    gin_hbm,
    gout_hbm,
    gsmall_ref,
    xloc,
    small_src,
    small_all,
    wf,
    wh,
    wl,
    par,
    ktab,
    hid,
    cotb,
    zn,
    zh,
    zl,
    raw,
    xs,
    ybuf,
    actp,
    dyf,
    dyh,
    dyl,
    seed,
    gadj,
    dz,
    dh,
    gl,
    gsib,
    gblk,
    psum,
    gz,
    fin,
    s0_own,
    s0_sib,
    s0_z,
    s0_b,
    st_own,
    st_sib,
    st_src,
    st_buf,
    st_tot,
    cy_src,
    cy_buf,
    q_own,
    q_sib,
    q_blk,
    q_z,
    sem,
):
    nb, nz, seqs, tokens, feats, states, token_count = sizes
    nch = nb * nz
    tc, fb, sb = tokens // nb, feats // nb, states // nb
    steps = tc // SUBS
    ng = states // LANES
    fl = feats // LANES
    b = lax.axis_index("blk")
    r = lax.axis_index("row")
    core = r % 2
    z = r // 2
    chip = b * nz + z
    sibling = (b, z * 2 + 1 - core)
    z_pair = (b, (z + 1 - 2 * (z % 2)) * 2 + core)
    blk_peers = [((b + k) % nb) for k in range(1, nb)]

    def several(count, body):
        if count <= 16:
            for k in range(1, count):
                body(k)
        else:

            def step(k, carry):
                body(k)
                return carry

            lax.fori_loop(1, count, step, 0)

    def over_z(body):
        def peer(k):
            q = (z + k) % nz
            body(q, (b, q * 2 + core))

        several(nz, peer)

    def over_chips(body):
        def peer(k):
            q = (chip + k) % nch
            body((q // nz, (q % nz) * 2 + core))

        several(nch, peer)

    barrier = pltpu.get_barrier_semaphore()
    pl.semaphore_signal(barrier, 1, device_id=sibling, device_id_type=MESH)
    over_chips(
        lambda dev: pl.semaphore_signal(barrier, 1, device_id=dev, device_id_type=MESH)
    )

    slots = iter(range(SEMAPHORES))
    sent = []

    def new():
        return next(slots)

    def start(src, dst, pair, dev):
        pltpu.make_async_remote_copy(
            src, dst, sem.at[pair[0]], sem.at[pair[1]], device_id=dev, device_id_type=MESH
        ).start()

    def take(ref, slot):
        pltpu.make_async_copy(ref, ref, sem.at[slot]).wait()

    def near(src, dst, slot):
        pltpu.make_async_copy(src, dst, sem.at[slot]).start()

    def near_done(ref, slot):
        pltpu.make_async_copy(ref, ref, sem.at[slot]).wait()

    def rows_of(i, size):
        return pl.ds(pl.multiple_of(i * size, size), size)

    def rows_at(i, size):
        return pl.ds(pl.multiple_of(i, 8), size)

    def to_sibling(src, dst, total=None):
        pair = (new(), new())
        start(src, dst, pair, sibling)
        sent.append((src, pair[0]))
        return pair

    def to_blk(make, total):
        pair = (new(), new())
        for p in blk_peers:
            start(*make(p), pair, (p, r))
        sent.append((total, pair[0]))
        return pair

    def to_z(make, total):
        pair = (new(), new())
        over_z(lambda p, dev: start(*make(p), pair, dev))
        sent.append((total, pair[0]))
        return pair

    my_cols = rows_of(b, fb)
    mats = [in_hbm if kind == "in" else out_mat_hbm for _, kind in MATRICES]
    x_slot, h_slot, c_slot = new(), new(), new()
    own_slots = [new() for _ in MATRICES]
    near(x_hbm, xloc, x_slot)
    near(x_hbm.at[rows_of(b, tc), :], hid.at[0, :, my_cols], h_slot)
    near(cot_hbm.at[rows_of(b, tc), :], cotb.at[:, my_cols], c_slot)
    for m, (layer, _) in enumerate(MATRICES):
        for part in range(2):
            near(
                mats[m].at[layer, part],
                wf.at[m, rows_at(part * states + b * sb, sb), :],
                own_slots[m],
            )

    small_src[...] = jnp.zeros_like(small_src)
    for layer in range(2):
        small_src[2 * layer : 2 * layer + 2, 0:sb] = poles_ref[layer]
    small_src[4:6, 0:sb] = step_ref[...]
    small_src[6:8, :] = feed_ref[...]
    small_src[8:10, :] = gain_ref[...]
    small_src[10:12, :] = bias_ref[...]
    small_all[b] = small_src[...]
    pl.semaphore_wait(barrier, nch)

    shared = [s and nz % 2 == 0 for s in SHARED]
    piece_rows = [sb // 2 if s else sb for s in shared]
    fetched = [wf.at[m, 0 : (nb - 1) * piece_rows[m], :] for m in range(4)]
    blk_pairs, z_pairs, near_pairs, far_pairs = {}, {}, {}, {}

    def weight_piece(m, p, other=False):
        half = (z % 2) * piece_rows[m] if shared[m] else 0
        if other:
            half = (1 - z % 2) * piece_rows[m]
        return wf.at[m, rows_at(core * states + p * sb + half, piece_rows[m]), :]

    def fetch(m):
        half = (z % 2) * piece_rows[m] if shared[m] else 0
        src = mats[m].at[MATRICES[m][0], core, rows_at(half, piece_rows[m]), :]
        blk_pairs[m] = to_blk(lambda p: (src, weight_piece(m, b)), fetched[m])

    def relay(m):
        take(fetched[m], blk_pairs[m][1])
        near_pairs[m] = (new(), new())
        if shared[m]:
            z_pairs[m] = (new(), new())
            sent.append((fetched[m], z_pairs[m][0]))
        for p in blk_peers:
            piece = weight_piece(m, p)
            if shared[m]:
                start(piece, piece, z_pairs[m], z_pair)
            start(piece, piece, near_pairs[m], sibling)
        sent.append((fetched[m], near_pairs[m][0]))

    def relay_far(m):
        if shared[m]:
            take(fetched[m], z_pairs[m][1])
            far_pairs[m] = (new(), new())
            for p in blk_peers:
                piece = weight_piece(m, p, other=True)
                start(piece, piece, far_pairs[m], sibling)
            sent.append((fetched[m], far_pairs[m][0]))

    def split_matrix(m):
        near_done(wf.at[m, 0 : 2 * sb, :], own_slots[m])
        take(fetched[m], near_pairs[m][1])
        if shared[m]:
            take(fetched[m], far_pairs[m][1])
        scaled = MATRICES[m][1] == "out"

        def body(i, carry):
            rows = rows_of(i, 64)
            values = wf[m, rows, :]
            if scaled:
                values = values * jnp.where(i * 64 < states, 2.0, -2.0)
            wh[m, rows, :], wl[m, rows, :] = halves(values)
            return carry

        lax.fori_loop(0, 2 * states // 64, body, 0)

    def spread_in(src, dst, low, count):
        total = dst.at[low : low + count, 0 : (nb - 1) * fb]
        pair = to_blk(
            lambda p: (
                src.at[rows_at(p * tc + low, count), :],
                dst.at[low : low + count, my_cols],
            ),
            total,
        )
        return total, pair[1]

    def spread_out(src, dst, low, count):
        slot = new()
        mine = dst.at[rows_at(b * tc + low, count), :]
        near(src.at[low : low + count, my_cols], mine, slot)
        total = dst.at[0 : (nb - 1) * count, :]
        pair = to_blk(lambda p: (src.at[low : low + count, rows_of(p, fb)], mine), total)
        return (total, pair[1]), (mine, slot)

    small_total = small_all.at[0 : nb - 1]
    small_pair = to_blk(lambda p: (small_src, small_all.at[b]), small_total)
    fetch(0)
    x_total, x_arrival = spread_in(x_hbm, hid.at[0], 0, tc)
    near_done(xloc, x_slot)

    def add_rows(i, carry):
        total, square = carry
        values = xloc[rows_of(i, 64), :].reshape(8, SUBS, fb)
        return total + jnp.sum(values, axis=0), square + jnp.sum(values * values, axis=0)

    zero_tile = jnp.zeros((SUBS, fb), F32)
    total, square = lax.fori_loop(0, tokens // 64, add_rows, (zero_tile, zero_tile))
    s0_own[...] = jnp.zeros_like(s0_own)
    s0_own[0:1, :] = jnp.sum(total, axis=0, keepdims=True)
    s0_own[1:2, :] = jnp.sum(square, axis=0, keepdims=True)
    s0_pair = to_sibling(s0_own, s0_sib)
    starts = [jnp.int32(0)]
    for i in range(seqs - 1):
        starts.append(starts[-1] + seq_ref[0, i])
    begins = starts
    ends = starts[1:] + [jnp.int32(tokens)]

    def none_in(low, size, marks, shift):
        hit = None
        for mark in marks:
            at = mark - shift - low
            inside = jnp.logical_and(at >= 0, at < size)
            hit = inside if hit is None else jnp.logical_or(hit, inside)
        return jnp.where(hit, 0.0, 1.0).astype(F32)

    sub_index = lax.broadcasted_iota(jnp.int32, (SUBS, LANES), 0)
    base = b * tc
    marks = ((begins, 0), (ends, 1))

    def fill_flags(k, carry):
        for way in range(2):
            ktab[way, k] = none_in(base + sub_index * steps + k, 1, *marks[way])
        return carry

    lax.fori_loop(0, steps, fill_flags, 0)
    whole_sub = [none_in(base + sub_index * steps, steps, *marks[way]) for way in range(2)]
    whole_chunk = [[none_in(p * tc, tc, *marks[way]) for p in range(nb)] for way in range(2)]

    take(s0_sib, s0_pair[1])
    s0_z[z] = s0_own[...] + s0_sib[...]
    s0_total = s0_z.at[0 : nz - 1]
    s0_pair = to_z(lambda p: (s0_z.at[z], s0_z.at[z]), s0_total)

    take(small_total, small_pair[1])
    state_rows = jnp.concatenate([small_all[p][0:8, 0:sb] for p in range(nb)], axis=1)

    def feature_row(row):
        return jnp.concatenate([small_all[p][row : row + 1, :] for p in range(nb)], axis=1)

    def discretize(real, imag, log_step):
        step = jnp.exp(log_step)
        magnitude = jnp.exp(real * step)
        lr = magnitude * jnp.cos(imag * step)
        li = magnitude * jnp.sin(imag * step)
        modulus = real * real + imag * imag
        fr = ((lr - 1.0) * real + li * imag) / modulus
        fi = (li * real - (lr - 1.0) * imag) / modulus
        return step, lr, li, fr, fi, modulus

    for layer in range(2):
        _, lr, li, fr, fi, _ = discretize(
            state_rows[2 * layer : 2 * layer + 1, :],
            state_rows[2 * layer + 1 : 2 * layer + 2, :],
            state_rows[4 + layer : 5 + layer, :],
        )
        power = [(lr, li)]
        size = 1
        while size < tc:
            power.append(cmul(*power[-1], *power[-1]))
            size *= 2
        at_steps = power[steps.bit_length() - 1]
        for row, value in enumerate((lr, li, fr, fi, *at_steps, *power[-1])):
            par[layer, row : row + 1, :] = value

    def wide(layer, row, group):
        part = par[layer, row : row + 1, group * LANES : (group + 1) * LANES]
        return jnp.broadcast_to(part, (SUBS, LANES))

    take(s0_total, s0_pair[1])
    s0_b[b] = jnp.sum(s0_z[...], axis=0)
    s0_total = s0_b.at[0 : nb - 1]
    s0_pair = to_blk(lambda p: (s0_b.at[b], s0_b.at[b]), s0_total)
    fetch(1)
    relay(0)

    def load(ref, g, k):
        return ref[g, pl.ds(k, SUBS, stride=steps), :]

    def recur(carry, keep, lam, pushes):
        gated = [c * keep for c in carry]
        new = []
        for g in range(ng):
            vr, vi = cmul(lam[0][g], lam[1][g], gated[g], gated[ng + g])
            new.append((vr + pushes[g], vi + pushes[ng + g]))
        return gated, [v[0] for v in new] + [v[1] for v in new]

    def scan_local(src, lam, way, reverse):
        def body(i, carry):
            k = steps - 1 - i if reverse else i
            pushes = [load(src, g, k) for g in range(2 * ng)]
            return tuple(recur(carry, ktab[way, k], lam, pushes)[1])

        zero = jnp.zeros((SUBS, LANES), F32)
        return lax.fori_loop(0, steps, body, (zero,) * (2 * ng), unroll=4)

    def prefix(last, power, way, reverse):
        out = []
        for g in range(ng):
            sr, si = last[g], last[ng + g]
            ar, ai = power[0][g] * whole_sub[way], power[1][g] * whole_sub[way]
            for d in (1, 2, 4):
                shift = SUBS - d if reverse else d
                ok = sub_index < SUBS - d if reverse else sub_index >= d
                tr, ti = cmul(ar, ai, pltpu.roll(sr, shift, 0), pltpu.roll(si, shift, 0))
                br, bi = cmul(ar, ai, pltpu.roll(ar, shift, 0), pltpu.roll(ai, shift, 0))
                sr, si = jnp.where(ok, sr + tr, sr), jnp.where(ok, si + ti, si)
                ar, ai = jnp.where(ok, br, ar), jnp.where(ok, bi, ai)
            out.append((sr, si, ar, ai))
        return out

    carry_pairs = {}

    def send_carry(e, pre, reverse):
        row = 0 if reverse else SUBS - 1
        for g in range(ng):
            cols = slice(g * LANES, (g + 1) * LANES)
            for part in range(2):
                cy_src[e, part : part + 1, cols] = pre[g][part][row : row + 1, :]
                cy_buf[e, b, part : part + 1, cols] = pre[g][part][row : row + 1, :]
        carry_pairs[e] = to_blk(
            lambda p: (cy_src.at[e], cy_buf.at[e, b]), cy_buf.at[e, 0 : nb - 1]
        )

    def take_carry(e, pre, layer, way, reverse, sign):
        take(cy_buf.at[e, 0 : nb - 1], carry_pairs[e][1])
        ar, ai = par[layer, 6:7, :], sign * par[layer, 7:8, :]
        zero = jnp.zeros((1, states), F32)
        cr, ci, er, ei = zero, zero, zero, zero
        for p in reversed(range(nb)) if reverse else range(nb):
            er, ei = jnp.where(b == p, cr, er), jnp.where(b == p, ci, ei)
            tr, ti = cmul(ar, ai, cr, ci)
            keep = whole_chunk[way][p]
            cr = cy_buf[e, p, 0:1, :] + keep * tr
            ci = cy_buf[e, p, 1:2, :] + keep * ti
        shift = SUBS - 1 if reverse else 1
        first = sub_index == (SUBS - 1 if reverse else 0)
        carry_r, carry_i = [], []
        for g in range(ng):
            cols = slice(g * LANES, (g + 1) * LANES)
            wr = jnp.broadcast_to(er[:, cols], (SUBS, LANES))
            wi = jnp.broadcast_to(ei[:, cols], (SUBS, LANES))
            sr, si, dr, di = (pltpu.roll(v, shift, 0) for v in pre[g])
            tr, ti = cmul(dr, di, wr, wi)
            carry_r.append(jnp.where(first, wr, sr + tr))
            carry_i.append(jnp.where(first, wi, si + ti))
        return tuple(carry_r + carry_i)

    def forward_states(layer, carry, way, reverse, lam):
        scale = [[wide(layer, 2 + part, g) for g in range(ng)] for part in range(2)]
        src, dst = raw.at[layer], xs.at[layer]

        def body(i, carry):
            k = steps - 1 - i if reverse else i
            pushes = [load(src, g, k) for g in range(2 * ng)]
            _, new = recur(carry, ktab[way, k], lam, pushes)
            for g in range(ng):
                vr, vi = cmul(scale[0][g], scale[1][g], new[g], new[ng + g])
                dst[g, pl.ds(k, SUBS, stride=steps), :] = vr
                dst[ng + g, pl.ds(k, SUBS, stride=steps), :] = vi
            return tuple(new)

        lax.fori_loop(0, steps, body, carry, unroll=4)

    def adjoint_states(layer, carry, way, reverse, lam):
        scale = [[wide(layer, 2 + part, g) for g in range(ng)] for part in range(2)]
        zero = jnp.zeros((SUBS, LANES), F32)

        def body(i, loop):
            carry, sums = loop
            k = steps - 1 - i if reverse else i
            at = pl.ds(k, SUBS, stride=steps)
            pushes = [load(seed, g, k) for g in range(2 * ng)]
            gated, new = recur(carry, ktab[way, k], lam, pushes)
            sums = list(sums)
            for g in range(ng):
                xr, xi = xs[layer, g, at, :], xs[layer, ng + g, at, :]
                ur, ui = raw[layer, g, at, :], raw[layer, ng + g, at, :]
                pr, pi = gated[g], gated[ng + g]
                vr, vi = new[g], new[ng + g]
                sums[g] += pr * xr + pi * xi
                sums[ng + g] += pi * xr - pr * xi
                sums[2 * ng + g] += vr * ur + vi * ui
                sums[3 * ng + g] += vi * ur - vr * ui
                gadj[g, at, :] = scale[0][g] * vr + scale[1][g] * vi
                gadj[ng + g, at, :] = scale[0][g] * vi - scale[1][g] * vr
            return tuple(new), tuple(sums)

        return lax.fori_loop(0, steps, body, (carry, (zero,) * (4 * ng)), unroll=4)[1]

    tile = 256 if tc % 256 == 0 else tc

    def to_groups(left, m, dst):
        def body(i, carry):
            rows = rows_of(i, tile)
            value = product(
                (left[0][rows, :], left[1][rows, :]), (wh[m], wl[m]), "nt"
            )
            for g in range(2 * ng):
                dst[g, rows, :] = value[:, g * LANES : (g + 1) * LANES]
            return carry

        lax.fori_loop(0, tc // tile, body, 0)

    def from_groups(src, m, dst):
        def body(i, carry):
            rows = rows_of(i, tile)
            left = jnp.concatenate([src[g, rows, :] for g in range(2 * ng)], axis=1)
            dst[rows, :] = product(halves(left), (wh[m], wl[m]), "nn")
            return carry

        lax.fori_loop(0, tc // tile, body, 0)

    def weight_grad(src, right, m, scaled):
        def body(pair, carry):
            left = jnp.concatenate([src[2 * pair], src[2 * pair + 1]], axis=1)
            value = product(halves(left), (right[0][...], right[1][...]), "tn")
            for half in range(2):
                g = 2 * pair + half
                part = value[half * LANES : (half + 1) * LANES, :]
                if scaled:
                    part = part * jnp.where(g < ng, 2.0, -2.0)
                gl[m, rows_of(g, LANES), :] = part
            return carry

        lax.fori_loop(0, ng, body, 0)

    stats_pairs = {}

    def stats_start(i, first, second):
        for n, value in enumerate((first, second)):
            for j in range(fl):
                row = n * fl + j
                st_own[i, row : row + 1, :] = value[:, j * LANES : (j + 1) * LANES]
        take(st_sib.at[i], to_sibling(st_own.at[i], st_sib.at[i])[1])
        both = st_own[i] + st_sib[i]
        st_src[i] = both
        st_buf[i, chip] = both
        stats_pairs[i] = (new(), new())
        over_chips(lambda dev: start(st_src.at[i], st_buf.at[i, chip], stats_pairs[i], dev))
        sent.append((st_buf.at[i, 0 : nch - 1], stats_pairs[i][0]))

    def stats_end(i):
        take(st_buf.at[i, 0 : nch - 1], stats_pairs[i][1])
        st_tot[i] = jnp.sum(st_buf[i], axis=0)
        return [
            jnp.concatenate(
                [st_tot[i, n * fl + j : n * fl + j + 1, :] for j in range(fl)], axis=1
            )
            for n in range(2)
        ]

    def to_row(value):
        return jnp.sum(value, axis=0, keepdims=True)

    def eights(value):
        return jnp.sum(value.reshape(value.shape[0] // SUBS, SUBS, feats), axis=0)

    gpair = {}
    pr = psum.shape[1] // nz

    def core_rows(part):
        return rows_at(part * states, states)

    def grad_core(m):
        gpair["core", m] = to_sibling(gl.at[m, core_rows(1 - core), :], gsib.at[m])

    def grad_add(m):
        take(gsib.at[m], gpair["core", m][1])

        def body(i, carry):
            gsib[m, rows_of(i, 32), :] += gl[m, rows_at(core * states + i * 32, 32), :]
            return carry

        lax.fori_loop(0, states // 32, body, 0)

    def grad_blk(m):
        gpair["blk", m] = to_blk(
            lambda p: (gsib.at[m, rows_at(p * sb, sb), :], gblk.at[m, b]),
            gblk.at[m, 0 : nb - 1],
        )

    def grad_z(m):
        take(gblk.at[m, 0 : nb - 1], gpair["blk", m][1])

        def body(i, carry):
            value = gsib[m, rows_at(b * sb + i * 8, 8), :]
            for p in blk_peers:
                value += gblk[m, p, rows_of(i, 8), :]
            for j in range(fl):
                psum[m, rows_at(j * sb + i * 8, 8), :] = value[:, j * LANES : (j + 1) * LANES]
            return carry

        lax.fori_loop(0, sb // 8, body, 0)
        gpair["z", m] = to_z(
            lambda p: (psum.at[m, rows_of(p, pr), :], gz.at[m, z]), gz.at[m, 0 : nz - 1]
        )

    def grad_gather(m):
        take(gz.at[m, 0 : nz - 1], gpair["z", m][1])
        mine = rows_of(z, pr)
        value = psum[m, mine, :]
        for p in range(nz):
            value += jnp.where(z == p, 0.0, gz[m, p])
        fin[m, core, mine, :] = value
        piece = fin.at[m, core, mine, :]
        gpair["all", m] = to_z(lambda p: (piece, piece), fin.at[m, core, 0 : (nz - 1) * pr, :])

    def grad_share(m):
        take(fin.at[m, core, 0 : (nz - 1) * pr, :], gpair["all", m][1])
        gpair["share", m] = to_sibling(fin.at[m, core], fin.at[m, core])

    stores = []

    def grad_store(m):
        take(fin.at[m, 1 - core], gpair["share", m][1])
        layer, kind = MATRICES[m]
        dst = (gin_hbm if kind == "in" else gout_hbm).at[layer]
        slot = new()
        for part in range(2):
            for j in range(fl):
                near(
                    fin.at[m, part, j * sb : (j + 1) * sb, :],
                    dst.at[part, :, j * LANES : (j + 1) * LANES],
                    slot,
                )
        stores.append((dst, slot))

    hc = tc // 2
    relay_far(0)
    split_matrix(0)
    take(s0_total, s0_pair[1])
    sums = [
        jnp.concatenate([s0_b[p][n : n + 1, :] for p in range(nb)], axis=1) for n in range(2)
    ]
    near_done(hid.at[0, :, my_cols], h_slot)
    take(x_total, x_arrival)

    scales = []
    small_rows = 32
    cot_parts = []

    for layer in range(2):
        way, reverse = layer, layer == 1
        mean = sums[0] / token_count
        rstd = lax.rsqrt(sums[1] / token_count - mean * mean + EPSILON)
        gain, bias, feed = (feature_row(row + layer) for row in (8, 10, 6))
        scales.append((rstd, gain, bias, feed))

        def normalize(i, carry, layer=layer, mean=mean, rstd=rstd, gain=gain, bias=bias):
            rows = rows_of(i, small_rows)
            unit = (hid[layer, rows, :] - mean) * rstd
            zn[layer, rows, :] = unit
            zh[layer, rows, :], zl[layer, rows, :] = halves(gain * unit + bias)
            return carry

        lax.fori_loop(0, tc // small_rows, normalize, 0)
        to_groups((zh.at[layer], zl.at[layer]), 2 * layer, raw.at[layer])
        if layer == 1:
            relay(3)
        lam = [[wide(layer, part, g) for g in range(ng)] for part in range(2)]
        power = [[wide(layer, 4 + part, g) for g in range(ng)] for part in range(2)]
        last = scan_local(raw.at[layer], lam, way, reverse)
        pre = prefix(last, power, way, reverse)
        send_carry(layer, pre, reverse)
        if layer == 0:
            fetch(2)
            relay(1)
            relay_far(1)
            split_matrix(1)
        else:
            cot_parts.append(spread_in(cot_hbm, cotb, hc, tc - hc))
            relay_far(3)
            split_matrix(3)
        carry = take_carry(layer, pre, layer, way, reverse, 1.0)
        forward_states(layer, carry, way, reverse, lam)
        if layer == 0:
            relay(2)
        from_groups(xs.at[layer], 2 * layer + 1, ybuf)

        def activate(i, carry, layer=layer, gain=gain, bias=bias, feed=feed):
            rows = rows_of(i, small_rows)
            mixed = ybuf[rows, :] + feed * (gain * zn[layer, rows, :] + bias)
            below = 0.5 * (1.0 + lax.erf(mixed * 0.7071067811865476))
            density = 0.3989422804014327 * jnp.exp(-0.5 * mixed * mixed)
            gate = 1.0 / (1.0 + jnp.exp(-mixed))
            gelu = mixed * below
            value = hid[layer, rows, :] + gelu * gate
            hid[layer + 1, rows, :] = value
            actp[layer, rows, :] = (below + mixed * density) * gate + gelu * gate * (1.0 - gate)
            return carry[0] + eights(value), carry[1] + eights(value * value)

        zero = jnp.zeros((SUBS, feats), F32)
        parts = lax.fori_loop(0, tc // small_rows, activate, (zero, zero))
        if layer == 0:
            stats_start(0, to_row(parts[0]), to_row(parts[1]))
            fetch(3)
            cot_parts.append(spread_in(cot_hbm, cotb, 0, hc))
            relay_far(2)
            split_matrix(2)
            sums = stats_end(0)

    near_done(cotb.at[:, my_cols], c_slot)
    for part in cot_parts:
        take(*part)
    outs = []
    for layer in (1, 0):
        way, reverse = 1 - layer, layer == 0
        rstd, gain, bias, feed = scales[layer]
        upper = cotb if layer == 1 else dh.at[0]

        def mixed_grad(i, carry, layer=layer, gain=gain, bias=bias, upper=upper):
            rows = rows_of(i, small_rows)
            value = upper[rows, :] * actp[layer, rows, :]
            dyf[rows, :] = value
            dyh[rows, :], dyl[rows, :] = halves(value)
            return carry + eights(value * (gain * zn[layer, rows, :] + bias))

        zero = jnp.zeros((SUBS, feats), F32)
        feed_grad = to_row(lax.fori_loop(0, tc // small_rows, mixed_grad, zero))
        to_groups((dyh, dyl), 2 * layer + 1, seed)
        lam = [
            [wide(layer, 0, g) for g in range(ng)],
            [-wide(layer, 1, g) for g in range(ng)],
        ]
        power = [
            [wide(layer, 4, g) for g in range(ng)],
            [-wide(layer, 5, g) for g in range(ng)],
        ]
        last = scan_local(seed, lam, way, reverse)
        pre = prefix(last, power, way, reverse)
        send_carry(2 + layer, pre, reverse)
        low = 0 if layer == 1 else hc
        outs.append(spread_out(hid.at[2], out_hbm, low, hc))
        weight_grad(xs.at[layer], (dyh, dyl), 2 * layer + 1, True)
        grad_core(2 * layer + 1)
        carry = take_carry(2 + layer, pre, layer, way, reverse, -1.0)
        state_sums = adjoint_states(layer, carry, way, reverse, lam)
        if layer == 0:
            grad_add(2)
            grad_z(3)
        grad_add(2 * layer + 1)
        from_groups(gadj, 2 * layer, dz)

        def dz_sums(i, carry, layer=layer, feed=feed):
            rows = rows_of(i, small_rows)
            value = dz[rows, :] + feed * dyf[rows, :]
            dz[rows, :] = value
            return carry[0] + eights(value), carry[1] + eights(value * zn[layer, rows, :])

        parts = lax.fori_loop(0, tc // small_rows, dz_sums, (zero, zero))
        stats_start(1 + layer, to_row(parts[0]), to_row(parts[1]))
        if layer == 1:
            grad_blk(3)
        else:
            grad_blk(2)
            grad_blk(1)
        weight_grad(gadj, (zh.at[layer], zl.at[layer]), 2 * layer, False)
        grad_core(2 * layer)
        for p in range(nb):
            q_own[p, layer : layer + 1, :] = feed_grad[:, p * fb : (p + 1) * fb]
        for n in range(4):
            vector = jnp.concatenate(
                [to_row(state_sums[n * ng + g]) for g in range(ng)], axis=1
            )
            row = 2 + 4 * layer + n
            for p in range(nb):
                q_own[p, row : row + 1, 0:sb] = vector[:, p * sb : (p + 1) * sb]
        if layer == 0:
            q_pair = to_sibling(q_own, q_sib)
            grad_gather(3)
            grad_add(0)
            grad_blk(0)
            take(q_sib, q_pair[1])
            q_sib[...] += q_own[...]
            q_total = q_blk.at[0 : nb - 1]
            q_pair = to_blk(lambda p: (q_sib.at[p], q_blk.at[b]), q_total)
        bias_grad, gain_grad = stats_end(1 + layer)

        def hidden_grad(
            i, carry, layer=layer, rstd=rstd, gain=gain, bias_grad=bias_grad, gain_grad=gain_grad, upper=upper
        ):
            rows = rows_of(i, small_rows)
            inner = (
                dz[rows, :]
                - bias_grad / token_count
                - zn[layer, rows, :] * (gain_grad / token_count)
            )
            dh[1 - layer, rows, :] = upper[rows, :] + gain * rstd * inner
            return carry

        lax.fori_loop(0, tc // small_rows, hidden_grad, 0)
        gsmall_ref[2 + layer : 3 + layer, :] = st_tot[1 + layer, pl.ds(fl + b, 1), :]
        gsmall_ref[4 + layer : 5 + layer, :] = st_tot[1 + layer, pl.ds(b, 1), :]

    outs.append(spread_out(dh.at[1], gx_hbm, 0, tc))
    grad_share(3)
    grad_z(2)
    grad_store(3)
    grad_z(1)
    grad_gather(2)
    grad_share(2)
    grad_gather(1)
    grad_store(2)
    grad_share(1)
    grad_z(0)
    take(q_total, q_pair[1])
    value = q_sib[b]
    for p in blk_peers:
        value += q_blk[p]
    q_z[z] = value
    q_total = q_z.at[0 : nz - 1]
    q_pair = to_z(lambda p: (q_z.at[z], q_z.at[z]), q_total)
    grad_store(1)
    grad_gather(0)
    take(q_total, q_pair[1])
    small = jnp.sum(q_z[...], axis=0)
    gsmall_ref[0:2, :] = small[0:2, :]
    for layer in range(2):
        real = poles_ref[layer, 0:1, :]
        imag = poles_ref[layer, 1:2, :]
        step, lr, li, fr, fi, modulus = discretize(real, imag, step_ref[layer : layer + 1, :])
        lgr, lgi, fgr, fgi = (
            small[2 + 4 * layer + n : 3 + 4 * layer + n, 0:sb] for n in range(4)
        )
        qr = (real * fgr - imag * fgi) / modulus
        qi = (real * fgi + imag * fgr) / modulus
        tr, ti = lgr + qr, lgi + qi
        wr = lr * tr + li * ti
        wi = lr * ti - li * tr
        row = 6 + 2 * layer
        gsmall_ref[row : row + 1, 0:sb] = step * wr - (fr * qr + fi * qi)
        gsmall_ref[row + 1 : row + 2, 0:sb] = step * wi - (fr * qi - fi * qr)
        gsmall_ref[10 + layer : 11 + layer, 0:sb] = step * (real * wr + imag * wi)
    grad_share(0)
    for arrival, mine in outs:
        take(*arrival)
        near_done(*mine)
    grad_store(0)
    for ref, slot in stores:
        near_done(ref, slot)
    for ref, slot in sent:
        take(ref, slot)


def finish(
    out_in, gx_in, gin_in, gout_in, small_in, out, gx, gpoles, gstep, gin, gout, gfeed, ggain, gbias, *scratch
):
    sem = scratch[-1]
    chunks = []
    for n, (src, dst, buf) in enumerate(zip((out_in, gx_in, gin_in, gout_in), (out, gx, gin, gout), scratch)):
        for half in range(2):
            if n < 2:
                rows = src.shape[0] // 2
                at = pl.ds(half * rows, rows)
            else:
                at = half
            chunks.append((src.at[at], buf.at[at], dst.at[at], sem.at[0, 2 * n + half], sem.at[1, 2 * n + half]))
    for src, buf, _, arrived, _ in chunks:
        pltpu.make_async_copy(src, buf, arrived).start()
    sb = gstep.shape[1]
    gfeed[...] = small_in[0:2, :]
    ggain[...] = small_in[2:4, :]
    gbias[...] = small_in[4:6, :]
    for layer in range(2):
        gpoles[layer] = small_in[6 + 2 * layer : 8 + 2 * layer, 0:sb]
    gstep[...] = small_in[10:12, 0:sb]
    for src, buf, dst, arrived, written in chunks:
        pltpu.make_async_copy(src, buf, arrived).wait()
        pltpu.make_async_copy(buf, dst, written).start()
    for _, buf, dst, _, written in chunks:
        pltpu.make_async_copy(buf, dst, written).wait()


def local(mesh, *args):
    inputs, seq_lengths = args[0], args[1]
    nb, nr = mesh.shape["blk"], mesh.shape["row"]
    nz = nr // 2
    tokens, fb = inputs.shape
    sb = args[2].shape[2]
    states, feats = sb * nb, fb * nb
    assert seq_lengths.shape[0] == 1 and nr % 2 == 0
    assert fb % LANES == 0 and states % LANES == 0 and 2 * feats == SUBS * LANES
    assert tokens % (nb * SUBS * SUBS) == 0 and sb % 16 == 0 and states % 64 == 0
    tc = tokens // nb
    steps = tc // SUBS
    assert steps & (steps - 1) == 0
    nch = nb * nz
    fl = feats // LANES
    ng2 = 2 * states // LANES
    piece = -(-fl * sb // (nz * SUBS)) * SUBS
    sizes = (nb, nz, seq_lengths.shape[1], tokens, feats, states, tokens * nr)
    vmem = lambda *shape: pltpu.VMEM(shape, F32)
    half = lambda *shape: pltpu.VMEM(shape, BF16)
    scratch = [
        vmem(tokens, fb),
        vmem(16, fb),
        vmem(nb, 16, fb),
        vmem(4, 2 * states, feats),
        half(4, 2 * states, feats),
        half(4, 2 * states, feats),
        vmem(2, 8, states),
        vmem(2, steps, SUBS, LANES),
        vmem(3, tc, feats),
        vmem(tc, feats),
        vmem(2, tc, feats),
        half(2, tc, feats),
        half(2, tc, feats),
        vmem(2, ng2, tc, LANES),
        vmem(2, ng2, tc, LANES),
        vmem(tc, feats),
        vmem(2, tc, feats),
        vmem(tc, feats),
        half(tc, feats),
        half(tc, feats),
        vmem(ng2, tc, LANES),
        vmem(ng2, tc, LANES),
        vmem(tc, feats),
        vmem(2, tc, feats),
        vmem(4, 2 * states, feats),
        vmem(4, states, feats),
        vmem(4, nb, sb, feats),
        vmem(4, nz * piece, LANES),
        vmem(4, nz, piece, LANES),
        vmem(4, 2, nz * piece, LANES),
        vmem(8, fb),
        vmem(8, fb),
        vmem(nz, 8, fb),
        vmem(nb, 8, fb),
        vmem(3, 8, LANES),
        vmem(3, 8, LANES),
        vmem(3, 8, LANES),
        vmem(3, nch, 8, LANES),
        vmem(3, 8, LANES),
        vmem(4, 8, states),
        vmem(4, nb, 8, states),
        vmem(nb, 16, fb),
        vmem(nb, 16, fb),
        vmem(nb, 16, fb),
        vmem(nz, 16, fb),
        pltpu.SemaphoreType.DMA((SEMAPHORES,)),
    ]
    shaped = lambda like: jax.ShapeDtypeStruct(like.shape, like.dtype)
    anywhere = pl.BlockSpec(memory_space=pl.ANY)
    fast = pl.BlockSpec(memory_space=pltpu.VMEM)
    raw = pl.pallas_call(
        functools.partial(kernel, sizes),
        name="s5_layers",
        out_shape=tuple(shaped(args[i]) for i in (0, 0, 4, 5)) + (jax.ShapeDtypeStruct((16, fb), F32),),
        in_specs=[
            anywhere,
            pl.BlockSpec(memory_space=pltpu.SMEM),
            fast,
            fast,
            anywhere,
            anywhere,
            fast,
            fast,
            fast,
            anywhere,
        ],
        out_specs=(anywhere,) * 4 + (fast,),
        scratch_shapes=scratch,
        compiler_params=pltpu.CompilerParams(
            collective_id=0, has_side_effects=True, vmem_limit_bytes=60 << 20
        ),
    )(*args)
    return pl.pallas_call(
        finish,
        name="results",
        out_shape=tuple(shaped(args[i]) for i in (0, 0, 2, 3, 4, 5, 6, 7, 8)),
        in_specs=[anywhere] * 4 + [fast],
        out_specs=(anywhere, anywhere, fast, fast, anywhere, anywhere, fast, fast, fast),
        scratch_shapes=[pltpu.VMEM(args[i].shape, F32) for i in (0, 0, 4, 5)]
        + [pltpu.SemaphoreType.DMA((2, 8))],
        compiler_params=pltpu.CompilerParams(vmem_limit_bytes=60 << 20),
    )(*raw)


def solution(mesh):
    by_state = (P(None, None, "blk"), P(None, "blk"), P(None, None, "blk", None), P(None, None, "blk", None))
    by_feature = (P(None, "blk"),) * 3
    tokens = P("row", "blk")
    return jax.shard_map(
        functools.partial(local, mesh),
        mesh=mesh,
        in_specs=(tokens, P("row", None), *by_state, *by_feature, tokens),
        out_specs=(tokens, tokens, *by_state, *by_feature),
        check_vma=False,
    )
```

time: 182 us -> 162 us (0.89)
  Pallas kernels: 171 us -> 161 us
  local copies, waits for them, and re-layouts: 8.66 us -> 0 us
    pallas_call x1, Pallas kernels: 171 us -> 156 us  [local(): pl.pallas_call(functools.partial(kernel, sizes), name='s5_layers', out_sh...]
    unnamed x25 -> x0, local copies, waits for them, and re-layouts: 8.66 us -> none
    pallas_call x0 -> x1, Pallas kernels: none -> 4.29 us  [local(): pl.pallas_call(finish, name='results', out_shape=tuple((shaped(args[i]) f...]
where the time goes in v2:
time: 162 us; the launch traced here: 161 us
  Pallas kernels  161 us (99%)
    pallas_call x1, Pallas kernels, local(): pl.pallas_call(functools.partial(kernel, sizes), name='s5_layers', out_sh...  156 us
    pallas_call x1, Pallas kernels, local(): pl.pallas_call(finish, name='results', out_shape=tuple((shaped(args[i]) f...  4.29 us

profile of v2, /device:TPU:0, one launch (start us, length us, event | category | flops | bytes accessed | tf_op | source)
XLA Modules:
  0.0 161.3 jit_solution(11813010596810247544)
XLA Ops:
  0.6 156.3 %s5_layers.1 = (f32[2048,128]{1,0:T(8,128)}, f32[2048,128]{1,0:T(8,128)}, f32[2,2,96,512]{3,2,1,0:T(8,128)}, f32[2,2,96,512]{3,2,1,0:T(8,128)}, f32[16,128]{1,0:T(8,128)}) custom-call(f32[2048,128]{1,0:T(8,128)} %x_hbm.1, s32[1,3]{1,0:T(1,128)} %seq_ref.1, f32[2,2,96]{2,1,0:T(2,128)} %poles_ref.1, f32[2,96]{1,0:T(2,128)} %step_ref.1, ...), custom_call_target="tpu_custom_call" | custom-call | tf_op jit(solution)/shard_map/s5_layers/pallas_call | solution.py:958
  157.0 4.3 %results.1 = (f32[2048,128]{1,0:T(8,128)}, f32[2048,128]{1,0:T(8,128)}, f32[2,2,96]{2,1,0:T(2,128)}, f32[2,96]{1,0:T(2,128)}, f32[2,2,96,512]{3,2,1,0:T(8,128)},...) custom-call(f32[2048,128]{1,0:T(8,128)} %get-tuple-element.14.out_in, ...), custom_call_target="tpu_custom_call" | custom-call | tf_op jit(solution)/shard_map/results/pallas_call | solution.py:980

commit v3 on v2

--- a/solution.py
+++ b/solution.py
@@ -11,6 +11,7 @@
 EPSILON = 1e-05
 LANES = 128
 SUBS = 8
+GROUP = 4
 MESH = pl.DeviceIdType.MESH
 F32 = jnp.float32
 BF16 = jnp.bfloat16
@@ -65,8 +66,11 @@
     wl,
     par,
     ktab,
+    xin,
     hid,
     cotb,
+    outb,
+    gxb,
     zn,
     zh,
     zl,
@@ -201,8 +205,8 @@
     x_slot, h_slot, c_slot = new(), new(), new()
     own_slots = [new() for _ in MATRICES]
     near(x_hbm, xloc, x_slot)
-    near(x_hbm.at[rows_of(b, tc), :], hid.at[0, :, my_cols], h_slot)
-    near(cot_hbm.at[rows_of(b, tc), :], cotb.at[:, my_cols], c_slot)
+    near(x_hbm.at[rows_of(b, tc), :], xin.at[b], h_slot)
+    near(cot_hbm.at[rows_of(b, tc), :], cotb.at[b], c_slot)
     for m, (layer, _) in enumerate(MATRICES):
         for part in range(2):
             near(
@@ -277,12 +281,9 @@
         lax.fori_loop(0, 2 * states // 64, body, 0)
 
     def spread_in(src, dst, low, count):
-        total = dst.at[low : low + count, 0 : (nb - 1) * fb]
+        total = dst.at[0 : nb - 1, low : low + count, :]
         pair = to_blk(
-            lambda p: (
-                src.at[rows_at(p * tc + low, count), :],
-                dst.at[low : low + count, my_cols],
-            ),
+            lambda p: (src.at[rows_at(p * tc + low, count), :], dst.at[b, low : low + count, :]),
             total,
         )
         return total, pair[1]
@@ -290,15 +291,15 @@
     def spread_out(src, dst, low, count):
         slot = new()
         mine = dst.at[rows_at(b * tc + low, count), :]
-        near(src.at[low : low + count, my_cols], mine, slot)
-        total = dst.at[0 : (nb - 1) * count, :]
-        pair = to_blk(lambda p: (src.at[low : low + count, rows_of(p, fb)], mine), total)
+        near(src.at[b, low : low + count, :], mine, slot)
+        total = src.at[0 : nb - 1, low : low + count, :]
+        pair = to_blk(lambda p: (src.at[p, low : low + count, :], mine), total)
         return (total, pair[1]), (mine, slot)
 
     small_total = small_all.at[0 : nb - 1]
     small_pair = to_blk(lambda p: (small_src, small_all.at[b]), small_total)
     fetch(0)
-    x_total, x_arrival = spread_in(x_hbm, hid.at[0], 0, tc)
+    x_total, x_arrival = spread_in(x_hbm, xin, 0, tc)
     near_done(xloc, x_slot)
 
     def add_rows(i, carry):
@@ -387,7 +388,26 @@
     relay(0)
 
     def load(ref, g, k):
-        return ref[g, pl.ds(k, SUBS, stride=steps), :]
+        return ref[rows_of(k, SUBS), g * LANES : (g + 1) * LANES]
+
+    def store(ref, g, k, value):
+        ref[rows_of(k, SUBS), g * LANES : (g + 1) * LANES] = value
+
+    def unpack(ref, i):
+        parts = [
+            jnp.concatenate(
+                [ref[j, pl.ds(i * GROUP + k, SUBS, stride=steps), :] for j in range(fl)], axis=1
+            )
+            for k in range(GROUP)
+        ]
+        return jnp.concatenate(parts, axis=0)
+
+    def pack(ref, i, value):
+        for k in range(GROUP):
+            for j in range(fl):
+                ref[j, pl.ds(i * GROUP + k, SUBS, stride=steps), :] = value[
+                    k * SUBS : (k + 1) * SUBS, j * LANES : (j + 1) * LANES
+                ]
 
     def recur(carry, keep, lam, pushes):
         gated = [c * keep for c in carry]
@@ -468,8 +488,8 @@
             _, new = recur(carry, ktab[way, k], lam, pushes)
             for g in range(ng):
                 vr, vi = cmul(scale[0][g], scale[1][g], new[g], new[ng + g])
-                dst[g, pl.ds(k, SUBS, stride=steps), :] = vr
-                dst[ng + g, pl.ds(k, SUBS, stride=steps), :] = vi
+                store(dst, g, k, vr)
+                store(dst, ng + g, k, vi)
             return tuple(new)
 
         lax.fori_loop(0, steps, body, carry, unroll=4)
@@ -481,21 +501,20 @@
         def body(i, loop):
             carry, sums = loop
             k = steps - 1 - i if reverse else i
-            at = pl.ds(k, SUBS, stride=steps)
             pushes = [load(seed, g, k) for g in range(2 * ng)]
             gated, new = recur(carry, ktab[way, k], lam, pushes)
             sums = list(sums)
             for g in range(ng):
-                xr, xi = xs[layer, g, at, :], xs[layer, ng + g, at, :]
-                ur, ui = raw[layer, g, at, :], raw[layer, ng + g, at, :]
+                xr, xi = load(xs.at[layer], g, k), load(xs.at[layer], ng + g, k)
+                ur, ui = load(raw.at[layer], g, k), load(raw.at[layer], ng + g, k)
                 pr, pi = gated[g], gated[ng + g]
                 vr, vi = new[g], new[ng + g]
                 sums[g] += pr * xr + pi * xi
                 sums[ng + g] += pi * xr - pr * xi
                 sums[2 * ng + g] += vr * ur + vi * ui
                 sums[3 * ng + g] += vi * ur - vr * ui
-                gadj[g, at, :] = scale[0][g] * vr + scale[1][g] * vi
-                gadj[ng + g, at, :] = scale[0][g] * vi - scale[1][g] * vr
+                store(gadj, g, k, scale[0][g] * vr + scale[1][g] * vi)
+                store(gadj, ng + g, k, scale[0][g] * vi - scale[1][g] * vr)
             return tuple(new), tuple(sums)
 
         return lax.fori_loop(0, steps, body, (carry, (zero,) * (4 * ng)), unroll=4)[1]
@@ -508,8 +527,7 @@
             value = product(
                 (left[0][rows, :], left[1][rows, :]), (wh[m], wl[m]), "nt"
             )
-            for g in range(2 * ng):
-                dst[g, rows, :] = value[:, g * LANES : (g + 1) * LANES]
+            dst[rows, :] = value
             return carry
 
         lax.fori_loop(0, tc // tile, body, 0)
@@ -517,15 +535,14 @@
     def from_groups(src, m, dst):
         def body(i, carry):
             rows = rows_of(i, tile)
-            left = jnp.concatenate([src[g, rows, :] for g in range(2 * ng)], axis=1)
-            dst[rows, :] = product(halves(left), (wh[m], wl[m]), "nn")
+            dst[rows, :] = product(halves(src[rows, :]), (wh[m], wl[m]), "nn")
             return carry
 
         lax.fori_loop(0, tc // tile, body, 0)
 
     def weight_grad(src, right, m, scaled):
         def body(pair, carry):
-            left = jnp.concatenate([src[2 * pair], src[2 * pair + 1]], axis=1)
+            left = src[:, pl.ds(pl.multiple_of(pair * 2 * LANES, 2 * LANES), 2 * LANES)]
             value = product(halves(left), (right[0][...], right[1][...]), "tn")
             for half in range(2):
                 g = 2 * pair + half
@@ -645,11 +662,11 @@
     sums = [
         jnp.concatenate([s0_b[p][n : n + 1, :] for p in range(nb)], axis=1) for n in range(2)
     ]
-    near_done(hid.at[0, :, my_cols], h_slot)
+    near_done(xin.at[b], h_slot)
     take(x_total, x_arrival)
 
     scales = []
-    small_rows = 32
+    small_rows = GROUP * SUBS
     cot_parts = []
 
     for layer in range(2):
@@ -661,7 +678,12 @@
 
         def normalize(i, carry, layer=layer, mean=mean, rstd=rstd, gain=gain, bias=bias):
             rows = rows_of(i, small_rows)
-            unit = (hid[layer, rows, :] - mean) * rstd
+            if layer == 0:
+                value = unpack(xin, i)
+                hid[0, rows, :] = value
+            else:
+                value = hid[1, rows, :]
+            unit = (value - mean) * rstd
             zn[layer, rows, :] = unit
             zh[layer, rows, :], zl[layer, rows, :] = halves(gain * unit + bias)
             return carry
@@ -698,7 +720,10 @@
             gate = 1.0 / (1.0 + jnp.exp(-mixed))
             gelu = mixed * below
             value = hid[layer, rows, :] + gelu * gate
-            hid[layer + 1, rows, :] = value
+            if layer == 0:
+                hid[1, rows, :] = value
+            else:
+                pack(outb, i, value)
             actp[layer, rows, :] = (below + mixed * density) * gate + gelu * gate * (1.0 - gate)
             return carry[0] + eights(value), carry[1] + eights(value * value)
 
@@ -712,18 +737,21 @@
             split_matrix(2)
             sums = stats_end(0)
 
-    near_done(cotb.at[:, my_cols], c_slot)
+    near_done(cotb.at[b], c_slot)
     for part in cot_parts:
         take(*part)
     outs = []
     for layer in (1, 0):
         way, reverse = 1 - layer, layer == 0
         rstd, gain, bias, feed = scales[layer]
-        upper = cotb if layer == 1 else dh.at[0]
+        upper = dh.at[layer]
 
         def mixed_grad(i, carry, layer=layer, gain=gain, bias=bias, upper=upper):
             rows = rows_of(i, small_rows)
-            value = upper[rows, :] * actp[layer, rows, :]
+            value = unpack(cotb, i) if layer == 1 else upper[rows, :]
+            if layer == 1:
+                upper[rows, :] = value
+            value = value * actp[layer, rows, :]
             dyf[rows, :] = value
             dyh[rows, :], dyl[rows, :] = halves(value)
             return carry + eights(value * (gain * zn[layer, rows, :] + bias))
@@ -743,7 +771,7 @@
         pre = prefix(last, power, way, reverse)
         send_carry(2 + layer, pre, reverse)
         low = 0 if layer == 1 else hc
-        outs.append(spread_out(hid.at[2], out_hbm, low, hc))
+        outs.append(spread_out(outb, out_hbm, low, hc))
         weight_grad(xs.at[layer], (dyh, dyl), 2 * layer + 1, True)
         grad_core(2 * layer + 1)
         carry = take_carry(2 + layer, pre, layer, way, reverse, -1.0)
@@ -798,14 +826,18 @@
                 - bias_grad / token_count
                 - zn[layer, rows, :] * (gain_grad / token_count)
             )
-            dh[1 - layer, rows, :] = upper[rows, :] + gain * rstd * inner
+            value = upper[rows, :] + gain * rstd * inner
+            if layer == 1:
+                dh[0, rows, :] = value
+            else:
+                pack(gxb, i, value)
             return carry
 
         lax.fori_loop(0, tc // small_rows, hidden_grad, 0)
         gsmall_ref[2 + layer : 3 + layer, :] = st_tot[1 + layer, pl.ds(fl + b, 1), :]
         gsmall_ref[4 + layer : 5 + layer, :] = st_tot[1 + layer, pl.ds(b, 1), :]
 
-    outs.append(spread_out(dh.at[1], gx_hbm, 0, tc))
+    outs.append(spread_out(gxb, gx_hbm, 0, tc))
     grad_share(3)
     grad_z(2)
     grad_store(3)
@@ -892,14 +924,13 @@
     sb = args[2].shape[2]
     states, feats = sb * nb, fb * nb
     assert seq_lengths.shape[0] == 1 and nr % 2 == 0
-    assert fb % LANES == 0 and states % LANES == 0 and 2 * feats == SUBS * LANES
+    assert fb == LANES and states % LANES == 0 and 2 * feats == SUBS * LANES
     assert tokens % (nb * SUBS * SUBS) == 0 and sb % 16 == 0 and states % 64 == 0
     tc = tokens // nb
     steps = tc // SUBS
     assert steps & (steps - 1) == 0
     nch = nb * nz
     fl = feats // LANES
-    ng2 = 2 * states // LANES
     piece = -(-fl * sb // (nz * SUBS)) * SUBS
     sizes = (nb, nz, seq_lengths.shape[1], tokens, feats, states, tokens * nr)
     vmem = lambda *shape: pltpu.VMEM(shape, F32)
@@ -913,20 +944,23 @@
         half(4, 2 * states, feats),
         vmem(2, 8, states),
         vmem(2, steps, SUBS, LANES),
-        vmem(3, tc, feats),
-        vmem(tc, feats),
+        vmem(nb, tc, fb),
+        vmem(2, tc, feats),
+        vmem(nb, tc, fb),
+        vmem(nb, tc, fb),
+        vmem(nb, tc, fb),
         vmem(2, tc, feats),
         half(2, tc, feats),
         half(2, tc, feats),
-        vmem(2, ng2, tc, LANES),
-        vmem(2, ng2, tc, LANES),
+        vmem(2, tc, 2 * states),
+        vmem(2, tc, 2 * states),
         vmem(tc, feats),
         vmem(2, tc, feats),
         vmem(tc, feats),
         half(tc, feats),
         half(tc, feats),
-        vmem(ng2, tc, LANES),
-        vmem(ng2, tc, LANES),
+        vmem(tc, 2 * states),
+        vmem(tc, 2 * states),
         vmem(tc, feats),
         vmem(2, tc, feats),
         vmem(4, 2 * states, feats),

time: 162 us -> 147 us (0.907)
  Pallas kernels: 161 us -> 146 us
    pallas_call x1, Pallas kernels: 156 us -> 141 us  [local(): pl.pallas_call(functools.partial(kernel, sizes), name='s5_layers', out_sh...]
where the time goes in v3:
time: 147 us; the launch traced here: 146 us
  Pallas kernels  146 us (99%)
    pallas_call x1, Pallas kernels, local(): pl.pallas_call(functools.partial(kernel, sizes), name='s5_layers', out_sh...  141 us
    pallas_call x1, Pallas kernels, local(): pl.pallas_call(finish, name='results', out_shape=tuple((shaped(args[i]) f...  4.29 us

profile of v3, /device:TPU:0, one launch (start us, length us, event | category | flops | bytes accessed | tf_op | source)
XLA Modules:
  0.0 146.3 jit_solution(10365335947142301478)
XLA Ops:
  0.6 141.3 %s5_layers.1 = (f32[2048,128]{1,0:T(8,128)}, f32[2048,128]{1,0:T(8,128)}, f32[2,2,96,512]{3,2,1,0:T(8,128)}, f32[2,2,96,512]{3,2,1,0:T(8,128)}, f32[16,128]{1,0:T(8,128)}) custom-call(f32[2048,128]{1,0:T(8,128)} %x_hbm.1, s32[1,3]{1,0:T(1,128)} %seq_ref.1, f32[2,2,96]{2,1,0:T(2,128)} %poles_ref.1, f32[2,96]{1,0:T(2,128)} %step_ref.1, ...), custom_call_target="tpu_custom_call" | custom-call | tf_op jit(solution)/shard_map/s5_layers/pallas_call | solution.py:992
  142.0 4.3 %results.1 = (f32[2048,128]{1,0:T(8,128)}, f32[2048,128]{1,0:T(8,128)}, f32[2,2,96]{2,1,0:T(2,128)}, f32[2,96]{1,0:T(2,128)}, f32[2,2,96,512]{3,2,1,0:T(8,128)},...) custom-call(f32[2048,128]{1,0:T(8,128)} %get-tuple-element.14.out_in, ...), custom_call_target="tpu_custom_call" | custom-call | tf_op jit(solution)/shard_map/results/pallas_call | solution.py:1014

commit v4 on v3

--- a/solution.py
+++ b/solution.py
@@ -17,7 +17,8 @@
 BF16 = jnp.bfloat16
 MATRICES = ((0, "in"), (0, "out"), (1, "in"), (1, "out"))
 SHARED = (True, False, True, True)
-SEMAPHORES = 128
+HALVED = (False, True, True, False)
+SEMAPHORES = 136
 DIMS = {
     "nt": (((1,), (1,)), ((), ())),
     "nn": (((1,), (0,)), ((), ())),
@@ -85,8 +86,8 @@
     gadj,
     dz,
     dh,
-    gl,
     gsib,
+    gpr,
     gblk,
     psum,
     gz,
@@ -385,6 +386,7 @@
     s0_total = s0_b.at[0 : nb - 1]
     s0_pair = to_blk(lambda p: (s0_b.at[b], s0_b.at[b]), s0_total)
     fetch(1)
+    fetch(2)
     relay(0)
 
     def load(ref, g, k):
@@ -603,34 +605,82 @@
 
         lax.fori_loop(0, states // 32, body, 0)
 
+    halved = [h and nz % 2 == 0 for h in HALVED]
+    grad_rows = [sb // 2 if h else sb for h in halved]
+    sharers = [nz // 2 if h else nz for h in halved]
+
+    def grad_piece(m, p, other=False):
+        low = p * sb
+        if halved[m]:
+            low = low + (1 - z % 2 if other else z % 2) * grad_rows[m]
+        return rows_at(low, grad_rows[m])
+
+    def grad_pair(m):
+        pair = (new(), new())
+        for p in range(nb):
+            start(gsib.at[m, grad_piece(m, p, True), :], gpr.at[m, p], pair, z_pair)
+        sent.append((gpr.at[m], pair[0]))
+        gpair["pair", m] = pair
+
+    def grad_pair_add(m):
+        take(gpr.at[m], gpair["pair", m][1])
+
+        def body(i, carry):
+            for p in range(nb):
+                low = p * sb + (z % 2) * grad_rows[m]
+                gsib[m, rows_at(low + i * 8, 8), :] += gpr[m, p, rows_of(i, 8), :]
+            return carry
+
+        lax.fori_loop(0, grad_rows[m] // 8, body, 0)
+
     def grad_blk(m):
         gpair["blk", m] = to_blk(
-            lambda p: (gsib.at[m, rows_at(p * sb, sb), :], gblk.at[m, b]),
-            gblk.at[m, 0 : nb - 1],
+            lambda p: (gsib.at[m, grad_piece(m, p), :], gblk.at[m, b, 0 : grad_rows[m], :]),
+            gblk.at[m, 0 : nb - 1, 0 : grad_rows[m], :],
         )
 
+    def my_sharers(m, body):
+        if halved[m]:
+            place = z // 2
+
+            def peer(k):
+                q = (place + k) % sharers[m]
+                body(q, (b, (q * 2 + z % 2) * 2 + core))
+
+            several(sharers[m], peer)
+        else:
+            over_z(body)
+
     def grad_z(m):
-        take(gblk.at[m, 0 : nb - 1], gpair["blk", m][1])
+        take(gblk.at[m, 0 : nb - 1, 0 : grad_rows[m], :], gpair["blk", m][1])
 
         def body(i, carry):
-            value = gsib[m, rows_at(b * sb + i * 8, 8), :]
+            low = b * sb + (z % 2) * grad_rows[m] if halved[m] else b * sb
+            value = gsib[m, rows_at(low + i * 8, 8), :]
             for p in blk_peers:
                 value += gblk[m, p, rows_of(i, 8), :]
             for j in range(fl):
-                psum[m, rows_at(j * sb + i * 8, 8), :] = value[:, j * LANES : (j + 1) * LANES]
+                psum[m, rows_at(j * grad_rows[m] + i * 8, 8), :] = value[
+                    :, j * LANES : (j + 1) * LANES
+                ]
             return carry
 
-        lax.fori_loop(0, sb // 8, body, 0)
-        gpair["z", m] = to_z(
-            lambda p: (psum.at[m, rows_of(p, pr), :], gz.at[m, z]), gz.at[m, 0 : nz - 1]
+        lax.fori_loop(0, grad_rows[m] // 8, body, 0)
+        place = z // 2 if halved[m] else z
+        pair = (new(), new())
+        my_sharers(
+            m, lambda q, dev: start(psum.at[m, rows_of(q, pr), :], gz.at[m, place], pair, dev)
         )
+        sent.append((gz.at[m, 0 : sharers[m] - 1], pair[0]))
+        gpair["z", m] = pair
 
     def grad_gather(m):
-        take(gz.at[m, 0 : nz - 1], gpair["z", m][1])
-        mine = rows_of(z, pr)
-        value = psum[m, mine, :]
-        for p in range(nz):
-            value += jnp.where(z == p, 0.0, gz[m, p])
+        take(gz.at[m, 0 : sharers[m] - 1], gpair["z", m][1])
+        place = z // 2 if halved[m] else z
+        value = psum[m, rows_of(place, pr), :]
+        for q in range(sharers[m]):
+            value += jnp.where(place == q, 0.0, gz[m, q])
+        mine = rows_of((z % 2) * sharers[m] + place if halved[m] else z, pr)
         fin[m, core, mine, :] = value
         piece = fin.at[m, core, mine, :]
         gpair["all", m] = to_z(lambda p: (piece, piece), fin.at[m, core, 0 : (nz - 1) * pr, :])
@@ -646,13 +696,16 @@
         layer, kind = MATRICES[m]
         dst = (gin_hbm if kind == "in" else gout_hbm).at[layer]
         slot = new()
+        count = grad_rows[m]
         for part in range(2):
-            for j in range(fl):
-                near(
-                    fin.at[m, part, j * sb : (j + 1) * sb, :],
-                    dst.at[part, :, j * LANES : (j + 1) * LANES],
-                    slot,
-                )
+            for h in range(sb // count):
+                for j in range(fl):
+                    low = h * sharers[m] * pr + j * count
+                    near(
+                        fin.at[m, part, low : low + count, :],
+                        dst.at[part, h * count : (h + 1) * count, j * LANES : (j + 1) * LANES],
+                        slot,
+                    )
         stores.append((dst, slot))
 
     hc = tc // 2
@@ -690,15 +743,13 @@
 
         lax.fori_loop(0, tc // small_rows, normalize, 0)
         to_groups((zh.at[layer], zl.at[layer]), 2 * layer, raw.at[layer])
-        if layer == 1:
-            relay(3)
         lam = [[wide(layer, part, g) for g in range(ng)] for part in range(2)]
         power = [[wide(layer, 4 + part, g) for g in range(ng)] for part in range(2)]
         last = scan_local(raw.at[layer], lam, way, reverse)
         pre = prefix(last, power, way, reverse)
         send_carry(layer, pre, reverse)
         if layer == 0:
-            fetch(2)
+            fetch(3)
             relay(1)
             relay_far(1)
             split_matrix(1)
@@ -731,12 +782,16 @@
         parts = lax.fori_loop(0, tc // small_rows, activate, (zero, zero))
         if layer == 0:
             stats_start(0, to_row(parts[0]), to_row(parts[1]))
-            fetch(3)
             cot_parts.append(spread_in(cot_hbm, cotb, 0, hc))
+            relay(3)
             relay_far(2)
             split_matrix(2)
             sums = stats_end(0)
 
+    for ref, slot in sent:
+        take(ref, slot)
+    sent.clear()
+    gl = wf
     near_done(cotb.at[b], c_slot)
     for part in cot_parts:
         take(*part)
@@ -770,15 +825,13 @@
         last = scan_local(seed, lam, way, reverse)
         pre = prefix(last, power, way, reverse)
         send_carry(2 + layer, pre, reverse)
-        low = 0 if layer == 1 else hc
-        outs.append(spread_out(outb, out_hbm, low, hc))
+        outs.append(spread_out(outb, out_hbm, 0 if layer == 1 else hc, hc))
         weight_grad(xs.at[layer], (dyh, dyl), 2 * layer + 1, True)
         grad_core(2 * layer + 1)
         carry = take_carry(2 + layer, pre, layer, way, reverse, -1.0)
+        if layer == 0:
+            grad_z(3)
         state_sums = adjoint_states(layer, carry, way, reverse, lam)
-        if layer == 0:
-            grad_add(2)
-            grad_z(3)
         grad_add(2 * layer + 1)
         from_groups(gadj, 2 * layer, dz)
 
@@ -790,11 +843,13 @@
 
         parts = lax.fori_loop(0, tc // small_rows, dz_sums, (zero, zero))
         stats_start(1 + layer, to_row(parts[0]), to_row(parts[1]))
-        if layer == 1:
-            grad_blk(3)
+        if layer == 0:
+            grad_pair_add(2)
+            grad_blk(2)
+        if halved[2 * layer + 1]:
+            grad_pair(2 * layer + 1)
         else:
-            grad_blk(2)
-            grad_blk(1)
+            grad_blk(2 * layer + 1)
         weight_grad(gadj, (zh.at[layer], zl.at[layer]), 2 * layer, False)
         grad_core(2 * layer)
         for p in range(nb):
@@ -806,11 +861,16 @@
             row = 2 + 4 * layer + n
             for p in range(nb):
                 q_own[p, row : row + 1, 0:sb] = vector[:, p * sb : (p + 1) * sb]
-        if layer == 0:
+        grad_add(2 * layer)
+        if layer == 1:
+            grad_pair(2)
+        else:
+            grad_blk(0)
             q_pair = to_sibling(q_own, q_sib)
             grad_gather(3)
-            grad_add(0)
-            grad_blk(0)
+            if halved[1]:
+                grad_pair_add(1)
+                grad_blk(1)
             take(q_sib, q_pair[1])
             q_sib[...] += q_own[...]
             q_total = q_blk.at[0 : nb - 1]
@@ -838,16 +898,12 @@
         gsmall_ref[4 + layer : 5 + layer, :] = st_tot[1 + layer, pl.ds(b, 1), :]
 
     outs.append(spread_out(gxb, gx_hbm, 0, tc))
+    grad_z(2)
     grad_share(3)
-    grad_z(2)
+    first, second = (0, 1) if halved[1] else (1, 0)
+    grad_z(first)
+    grad_gather(2)
     grad_store(3)
-    grad_z(1)
-    grad_gather(2)
-    grad_share(2)
-    grad_gather(1)
-    grad_store(2)
-    grad_share(1)
-    grad_z(0)
     take(q_total, q_pair[1])
     value = q_sib[b]
     for p in blk_peers:
@@ -855,8 +911,13 @@
     q_z[z] = value
     q_total = q_z.at[0 : nz - 1]
     q_pair = to_z(lambda p: (q_z.at[z], q_z.at[z]), q_total)
-    grad_store(1)
-    grad_gather(0)
+    grad_share(2)
+    grad_gather(first)
+    grad_z(second)
+    grad_store(2)
+    grad_share(first)
+    grad_gather(second)
+    grad_store(first)
     take(q_total, q_pair[1])
     small = jnp.sum(q_z[...], axis=0)
     gsmall_ref[0:2, :] = small[0:2, :]
@@ -876,32 +937,21 @@
         gsmall_ref[row : row + 1, 0:sb] = step * wr - (fr * qr + fi * qi)
         gsmall_ref[row + 1 : row + 2, 0:sb] = step * wi - (fr * qi - fi * qr)
         gsmall_ref[10 + layer : 11 + layer, 0:sb] = step * (real * wr + imag * wi)
-    grad_share(0)
     for arrival, mine in outs:
         take(*arrival)
         near_done(*mine)
-    grad_store(0)
+    grad_share(second)
+    grad_store(second)
     for ref, slot in stores:
         near_done(ref, slot)
     for ref, slot in sent:
         take(ref, slot)
 
 
-def finish(
-    out_in, gx_in, gin_in, gout_in, small_in, out, gx, gpoles, gstep, gin, gout, gfeed, ggain, gbias, *scratch
-):
-    sem = scratch[-1]
-    chunks = []
-    for n, (src, dst, buf) in enumerate(zip((out_in, gx_in, gin_in, gout_in), (out, gx, gin, gout), scratch)):
-        for half in range(2):
-            if n < 2:
-                rows = src.shape[0] // 2
-                at = pl.ds(half * rows, rows)
-            else:
-                at = half
-            chunks.append((src.at[at], buf.at[at], dst.at[at], sem.at[0, 2 * n + half], sem.at[1, 2 * n + half]))
-    for src, buf, _, arrived, _ in chunks:
-        pltpu.make_async_copy(src, buf, arrived).start()
+def finish(out_in, gx_in, gin_in, gout_in, small_in, out, gx, gpoles, gstep, gin, gout, gfeed, ggain, gbias, sem):
+    pairs = ((out_in, out), (gx_in, gx), (gin_in, gin), (gout_in, gout))
+    for n, (src, dst) in enumerate(pairs):
+        pltpu.make_async_copy(src, dst, sem.at[n]).start()
     sb = gstep.shape[1]
     gfeed[...] = small_in[0:2, :]
     ggain[...] = small_in[2:4, :]
@@ -909,11 +959,8 @@
     for layer in range(2):
         gpoles[layer] = small_in[6 + 2 * layer : 8 + 2 * layer, 0:sb]
     gstep[...] = small_in[10:12, 0:sb]
-    for src, buf, dst, arrived, written in chunks:
-        pltpu.make_async_copy(src, buf, arrived).wait()
-        pltpu.make_async_copy(buf, dst, written).start()
-    for _, buf, dst, _, written in chunks:
-        pltpu.make_async_copy(buf, dst, written).wait()
+    for n, (src, dst) in enumerate(pairs):
+        pltpu.make_async_copy(src, dst, sem.at[n]).wait()
 
 
 def local(mesh, *args):
@@ -963,8 +1010,8 @@
         vmem(tc, 2 * states),
         vmem(tc, feats),
         vmem(2, tc, feats),
-        vmem(4, 2 * states, feats),
         vmem(4, states, feats),
+        vmem(4, nb, sb // 2, feats),
         vmem(4, nb, sb, feats),
         vmem(4, nz * piece, LANES),
         vmem(4, nz, piece, LANES),
@@ -989,37 +1036,37 @@
     shaped = lambda like: jax.ShapeDtypeStruct(like.shape, like.dtype)
     anywhere = pl.BlockSpec(memory_space=pl.ANY)
     fast = pl.BlockSpec(memory_space=pltpu.VMEM)
+    main = pl.BlockSpec(memory_space=pltpu.HBM)
     raw = pl.pallas_call(
         functools.partial(kernel, sizes),
         name="s5_layers",
-        out_shape=tuple(shaped(args[i]) for i in (0, 0, 4, 5)) + (jax.ShapeDtypeStruct((16, fb), F32),),
+        out_shape=tuple(pltpu.VMEM(args[i].shape, F32) for i in (0, 0, 4, 5)) + (pltpu.VMEM((16, fb), F32),),
         in_specs=[
-            anywhere,
+            main,
             pl.BlockSpec(memory_space=pltpu.SMEM),
             fast,
             fast,
-            anywhere,
-            anywhere,
+            main,
+            main,
             fast,
             fast,
             fast,
-            anywhere,
+            main,
         ],
         out_specs=(anywhere,) * 4 + (fast,),
         scratch_shapes=scratch,
         compiler_params=pltpu.CompilerParams(
-            collective_id=0, has_side_effects=True, vmem_limit_bytes=60 << 20
+            collective_id=0, has_side_effects=True, vmem_limit_bytes=57 << 20
         ),
     )(*args)
     return pl.pallas_call(
         finish,
         name="results",
         out_shape=tuple(shaped(args[i]) for i in (0, 0, 2, 3, 4, 5, 6, 7, 8)),
-        in_specs=[anywhere] * 4 + [fast],
+        in_specs=[fast] * 5,
         out_specs=(anywhere, anywhere, fast, fast, anywhere, anywhere, fast, fast, fast),
-        scratch_shapes=[pltpu.VMEM(args[i].shape, F32) for i in (0, 0, 4, 5)]
-        + [pltpu.SemaphoreType.DMA((2, 8))],
-        compiler_params=pltpu.CompilerParams(vmem_limit_bytes=60 << 20),
+        scratch_shapes=[pltpu.SemaphoreType.DMA((4,))],
+        compiler_params=pltpu.CompilerParams(vmem_limit_bytes=8 << 20),
     )(*raw)
 
 

time: 147 us -> 134 us (0.912)
  Pallas kernels: 146 us -> 133 us
    pallas_call x1, Pallas kernels: 141 us -> 131 us  [local(): pl.pallas_call(functools.partial(kernel, sizes), name='s5_layers', out_sh...]
    pallas_call x1, Pallas kernels: 4.29 us -> 2.46 us  [local(): pl.pallas_call(finish, name='results', out_shape=tuple((shaped(args[i]) f...]
where the time goes in v4:
time: 134 us
  Pallas kernels  133 us (99%)
    pallas_call x1, Pallas kernels, local(): pl.pallas_call(functools.partial(kernel, sizes), name='s5_layers', out_sh...  131 us

profile of v4, /device:TPU:0, one launch (start us, length us, event | category | flops | bytes accessed | tf_op | source)
XLA Modules:
  0.0 133.7 jit_solution(16294647893741857058)
XLA Ops:
  0.6 130.6 %s5_layers.1 = (f32[2048,128]{1,0:T(8,128)S(1)}, f32[2048,128]{1,0:T(8,128)S(1)}, f32[2,2,96,512]{3,2,1,0:T(8,128)S(1)}, f32[2,2,96,512]{3,2,1,0:T(8,128)S(1)}, f32[16,128]{1,0:T(8,128)S(1)}) custom-call(f32[2048,128]{1,0:T(8,128)} %x_hbm.1, s32[1,3]{1,0:T(1,128)} %seq_ref.1, f32[2,2,96]{2,1,0:T(2,128)} %poles_ref.1, f32[2,96]{1,0:T(2,128)} %step_ref.1, ...), custom_call_target="tpu_custom_call" | custom-call | tf_op jit(solution)/shard_map/s5_layers/pallas_call | solution.py:1040
  131.3 2.5 %results.1 = (f32[2048,128]{1,0:T(8,128)}, f32[2048,128]{1,0:T(8,128)}, f32[2,2,96]{2,1,0:T(2,128)}, f32[2,96]{1,0:T(2,128)}, f32[2,2,96,512]{3,2,1,0:T(8,128)},...) custom-call(f32[2048,128]{1,0:T(8,128)S(1)} %get-tuple-element.14.out_in, ...), custom_call_target="tpu_custom_call" | custom-call | tf_op jit(solution)/shard_map/results/pallas_call | solution.py:1062

commit v5 on v4

--- a/solution.py
+++ b/solution.py
@@ -18,7 +18,7 @@
 MATRICES = ((0, "in"), (0, "out"), (1, "in"), (1, "out"))
 SHARED = (True, False, True, True)
 HALVED = (False, True, True, False)
-SEMAPHORES = 136
+SEMAPHORES = 132
 DIMS = {
     "nt": (((1,), (1,)), ((), ())),
     "nn": (((1,), (0,)), ((), ())),
@@ -444,17 +444,22 @@
         return out
 
     carry_pairs = {}
+    cy_src[...] = jnp.zeros_like(cy_src)
 
     def send_carry(e, pre, reverse):
         row = 0 if reverse else SUBS - 1
         for g in range(ng):
-            cols = slice(g * LANES, (g + 1) * LANES)
             for part in range(2):
-                cy_src[e, part : part + 1, cols] = pre[g][part][row : row + 1, :]
-                cy_buf[e, b, part : part + 1, cols] = pre[g][part][row : row + 1, :]
+                at = part * ng + g
+                cy_src[e, at : at + 1, :] = pre[g][part][row : row + 1, :]
+        cy_buf[e, b] = cy_src[e]
         carry_pairs[e] = to_blk(
             lambda p: (cy_src.at[e], cy_buf.at[e, b]), cy_buf.at[e, 0 : nb - 1]
         )
+
+    def carry_row(e, p, part):
+        rows = range(part * ng, (part + 1) * ng)
+        return jnp.concatenate([cy_buf[e, p, at : at + 1, :] for at in rows], axis=1)
 
     def take_carry(e, pre, layer, way, reverse, sign):
         take(cy_buf.at[e, 0 : nb - 1], carry_pairs[e][1])
@@ -465,8 +470,8 @@
             er, ei = jnp.where(b == p, cr, er), jnp.where(b == p, ci, ei)
             tr, ti = cmul(ar, ai, cr, ci)
             keep = whole_chunk[way][p]
-            cr = cy_buf[e, p, 0:1, :] + keep * tr
-            ci = cy_buf[e, p, 1:2, :] + keep * ti
+            cr = carry_row(e, p, 0) + keep * tr
+            ci = carry_row(e, p, 1) + keep * ti
         shift = SUBS - 1 if reverse else 1
         first = sub_index == (SUBS - 1 if reverse else 0)
         carry_r, carry_i = [], []
@@ -843,12 +848,12 @@
 
         parts = lax.fori_loop(0, tc // small_rows, dz_sums, (zero, zero))
         stats_start(1 + layer, to_row(parts[0]), to_row(parts[1]))
+        if halved[2 * layer + 1]:
+            grad_pair(2 * layer + 1)
         if layer == 0:
             grad_pair_add(2)
             grad_blk(2)
-        if halved[2 * layer + 1]:
-            grad_pair(2 * layer + 1)
-        else:
+        if not halved[2 * layer + 1]:
             grad_blk(2 * layer + 1)
         weight_grad(gadj, (zh.at[layer], zl.at[layer]), 2 * layer, False)
         grad_core(2 * layer)
@@ -868,14 +873,13 @@
             grad_blk(0)
             q_pair = to_sibling(q_own, q_sib)
             grad_gather(3)
-            if halved[1]:
-                grad_pair_add(1)
-                grad_blk(1)
             take(q_sib, q_pair[1])
             q_sib[...] += q_own[...]
             q_total = q_blk.at[0 : nb - 1]
             q_pair = to_blk(lambda p: (q_sib.at[p], q_blk.at[b]), q_total)
         bias_grad, gain_grad = stats_end(1 + layer)
+        if layer == 0:
+            grad_z(2)
 
         def hidden_grad(
             i, carry, layer=layer, rstd=rstd, gain=gain, bias_grad=bias_grad, gain_grad=gain_grad, upper=upper
@@ -897,12 +901,14 @@
         gsmall_ref[2 + layer : 3 + layer, :] = st_tot[1 + layer, pl.ds(fl + b, 1), :]
         gsmall_ref[4 + layer : 5 + layer, :] = st_tot[1 + layer, pl.ds(b, 1), :]
 
+    if halved[1]:
+        grad_pair_add(1)
+        grad_blk(1)
     outs.append(spread_out(gxb, gx_hbm, 0, tc))
-    grad_z(2)
     grad_share(3)
+    grad_gather(2)
     first, second = (0, 1) if halved[1] else (1, 0)
     grad_z(first)
-    grad_gather(2)
     grad_store(3)
     take(q_total, q_pair[1])
     value = q_sib[b]
@@ -911,12 +917,12 @@
     q_z[z] = value
     q_total = q_z.at[0 : nz - 1]
     q_pair = to_z(lambda p: (q_z.at[z], q_z.at[z]), q_total)
+    grad_z(second)
+    grad_gather(first)
     grad_share(2)
-    grad_gather(first)
-    grad_z(second)
+    grad_gather(second)
     grad_store(2)
     grad_share(first)
-    grad_gather(second)
     grad_store(first)
     take(q_total, q_pair[1])
     small = jnp.sum(q_z[...], axis=0)
@@ -975,7 +981,7 @@
     assert tokens % (nb * SUBS * SUBS) == 0 and sb % 16 == 0 and states % 64 == 0
     tc = tokens // nb
     steps = tc // SUBS
-    assert steps & (steps - 1) == 0
+    assert steps & (steps - 1) == 0 and 2 * states <= SUBS * LANES
     nch = nb * nz
     fl = feats // LANES
     piece = -(-fl * sb // (nz * SUBS)) * SUBS
@@ -1025,8 +1031,8 @@
         vmem(3, 8, LANES),
         vmem(3, nch, 8, LANES),
         vmem(3, 8, LANES),
-        vmem(4, 8, states),
-        vmem(4, nb, 8, states),
+        vmem(4, SUBS, LANES),
+        vmem(4, nb, SUBS, LANES),
         vmem(nb, 16, fb),
         vmem(nb, 16, fb),
         vmem(nb, 16, fb),

time: 134 us -> 129 us (0.963)
  Pallas kernels: 133 us -> 128 us
    pallas_call x1, Pallas kernels: 131 us -> 126 us  [local(): pl.pallas_call(functools.partial(kernel, sizes), name='s5_layers', out_sh...]
where the time goes in v5:
time: 129 us
  Pallas kernels  128 us (99%)
    pallas_call x1, Pallas kernels, local(): pl.pallas_call(functools.partial(kernel, sizes), name='s5_layers', out_sh...  126 us

profile of v5, /device:TPU:0, one launch (start us, length us, event | category | flops | bytes accessed | tf_op | source)
XLA Modules:
  0.0 129.1 jit_solution(8507522939828955771)
XLA Ops:
  0.6 126.0 %s5_layers.1 = (f32[2048,128]{1,0:T(8,128)S(1)}, f32[2048,128]{1,0:T(8,128)S(1)}, f32[2,2,96,512]{3,2,1,0:T(8,128)S(1)}, f32[2,2,96,512]{3,2,1,0:T(8,128)S(1)}, f32[16,128]{1,0:T(8,128)S(1)}) custom-call(f32[2048,128]{1,0:T(8,128)} %x_hbm.1, s32[1,3]{1,0:T(1,128)} %seq_ref.1, f32[2,2,96]{2,1,0:T(2,128)} %poles_ref.1, f32[2,96]{1,0:T(2,128)} %step_ref.1, ...), custom_call_target="tpu_custom_call" | custom-call | tf_op jit(solution)/shard_map/s5_layers/pallas_call | solution.py:1046
  126.6 2.5 %results.1 = (f32[2048,128]{1,0:T(8,128)}, f32[2048,128]{1,0:T(8,128)}, f32[2,2,96]{2,1,0:T(2,128)}, f32[2,96]{1,0:T(2,128)}, f32[2,2,96,512]{3,2,1,0:T(8,128)},...) custom-call(f32[2048,128]{1,0:T(8,128)S(1)} %get-tuple-element.14.out_in, ...), custom_call_target="tpu_custom_call" | custom-call | tf_op jit(solution)/shard_map/results/pallas_call | solution.py:1068

commit v6 on v5

--- a/solution.py
+++ b/solution.py
@@ -122,7 +122,10 @@
     chip = b * nz + z
     sibling = (b, z * 2 + 1 - core)
     z_pair = (b, (z + 1 - 2 * (z % 2)) * 2 + core)
-    blk_peers = [((b + k) % nb) for k in range(1, nb)]
+    if nb == 4:
+        blk_peers = [b + 1 - 2 * (b % 2), b + 2 - 4 * (b // 2), 3 - b]
+    else:
+        blk_peers = [(b + k) % nb for k in range(1, nb)]
 
     def several(count, body):
         if count <= 16:
@@ -144,11 +147,22 @@
         several(nz, peer)
 
     def over_chips(body):
-        def peer(k):
-            q = (chip + k) % nch
-            body((q // nz, (q % nz) * 2 + core))
-
-        several(nch, peer)
+        def peer(up, over):
+            body(((b + over) % nb, ((z + up) % nz) * 2 + core))
+
+        if nch <= 16:
+            for up in [*range(nz - 1, 0, -1), 0]:
+                for over in range(1, nb):
+                    peer(up, over)
+            for up in range(1, nz):
+                peer(up, 0)
+        else:
+
+            def step(k, carry):
+                peer(k % nz, k // nz)
+                return carry
+
+            lax.fori_loop(1, nch, step, 0)
 
     barrier = pltpu.get_barrier_semaphore()
     pl.semaphore_signal(barrier, 1, device_id=sibling, device_id_type=MESH)

time: 129 us -> 128 us (level)
    pallas_call x1, Pallas kernels: 126 us -> 124 us  [local(): pl.pallas_call(functools.partial(kernel, sizes), name='s5_layers', out_sh...]
where the time goes in v6:
time: 128 us; the launch traced here: 127 us
  Pallas kernels  127 us (99%)
    pallas_call x1, Pallas kernels, local(): pl.pallas_call(functools.partial(kernel, sizes), name='s5_layers', out_sh...  124 us

profile of v6, /device:TPU:0, one launch (start us, length us, event | category | flops | bytes accessed | tf_op | source)
XLA Modules:
  0.0 127.3 jit_solution(6569795123320309977)
XLA Ops:
  0.6 124.2 %s5_layers.1 = (f32[2048,128]{1,0:T(8,128)S(1)}, f32[2048,128]{1,0:T(8,128)S(1)}, f32[2,2,96,512]{3,2,1,0:T(8,128)S(1)}, f32[2,2,96,512]{3,2,1,0:T(8,128)S(1)}, f32[16,128]{1,0:T(8,128)S(1)}) custom-call(f32[2048,128]{1,0:T(8,128)} %x_hbm.1, s32[1,3]{1,0:T(1,128)} %seq_ref.1, f32[2,2,96]{2,1,0:T(2,128)} %poles_ref.1, f32[2,96]{1,0:T(2,128)} %step_ref.1, ...), custom_call_target="tpu_custom_call" | custom-call | tf_op jit(solution)/shard_map/s5_layers/pallas_call | solution.py:1060
  124.8 2.5 %results.1 = (f32[2048,128]{1,0:T(8,128)}, f32[2048,128]{1,0:T(8,128)}, f32[2,2,96]{2,1,0:T(2,128)}, f32[2,96]{1,0:T(2,128)}, f32[2,2,96,512]{3,2,1,0:T(8,128)},...) custom-call(f32[2048,128]{1,0:T(8,128)S(1)} %get-tuple-element.14.out_in, ...), custom_call_target="tpu_custom_call" | custom-call | tf_op jit(solution)/shard_map/results/pallas_call | solution.py:1082
